TPU v7x, 128 devices: a whole 4x4x4 slice. The times are simulated.
128 devices in a mesh: vocab: 32 (over z, y, core), tok: 4 (over x).
Axes of the slice: x: 4, y: 4, z: 4, core: 2. Of those that a mesh axis runs over, the one named last changes fastest.
Arguments:
- teacher_hidden: bfloat16 [512, 8192], P(None, 'tok'), may hold values from -80 to 80
- teacher_head: bfloat16 [8192, 81920], P('tok', 'vocab'), may hold values from -0.0625 to 0.0625
- student_hidden: bfloat16 [512, 3584], replicated, may hold values from -80 to 80
- student_head: bfloat16 [3584, 81920], P(None, ('vocab', 'tok')), may hold values from -0.09375 to 0.09375
- grammar_bits: int32 [512, 5120], P('tok', 'vocab'), may hold values from 0 to 65535
- sampled_ids: int32 [512], replicated, may hold values from 0 to 81919
Outputs:
- distill_loss: float32 [], replicated
- head_grad: bfloat16 [3584, 81920], P(None, ('vocab', 'tok'))
- hidden_grad: float32 [512, 3584], P(('vocab', 'tok'))
All inputs are finite; a program needn't handle non-finite values.
Results may differ from a plain program's by a relative error of at most 0.0038.
Values may be sent and summed in bfloat16 or wider, within the bound.
No kernel may reach another device: no remote copies, remote signals or barrier semaphores. Data moves between devices by JAX's collectives and lax.ppermute only.
A program may use at most 128 MiB of HBM per device.

v0:
```python
import jax
import jax.numpy as jnp
from jax import lax
from jax.experimental import pallas as pl
from jax.experimental.layout import Layout, with_layout_constraint
from jax.sharding import Mesh
from jax.sharding import PartitionSpec as P

sample_weight = 0.5
every_axis = ("z", "y", "c", "x")
wire = jnp.float16
hidden_scale = 1024.0


def device_of(z, y, c, x):
    return ((z % 4 * 4 + y % 4) * 2 + c % 2) * 4 + x % 4


def shift(value, z=0, y=0, c=0, x=0):
    pairs = [
        (device_of(k, j, i, h), device_of(k + z, j + y, i + c, h + x))
        for k in range(4)
        for j in range(4)
        for i in range(2)
        for h in range(4)
    ]
    return lax.ppermute(value, every_axis, pairs)


def wide(a):
    return a.astype(jnp.float32)


def row_major(a):
    return with_layout_constraint(a, Layout(major_to_minor=tuple(range(a.ndim))))


def head_kernel(hidden_ref, grad_ref, out_ref):
    out_ref[...] = lax.dot_general(
        hidden_ref[...],
        grad_ref[...],
        (((0,), (0,)), ((), ())),
        preferred_element_type=jnp.float32,
    ).astype(out_ref.dtype)


def head_product(hidden, grad):
    tokens, width = hidden.shape
    columns = grad.shape[1]
    step = width // 4
    return pl.pallas_call(
        head_kernel,
        grid=(4,),
        in_specs=[
            pl.BlockSpec((tokens, step), lambda i: (0, i)),
            pl.BlockSpec((tokens, columns), lambda i: (0, 0)),
        ],
        out_specs=pl.BlockSpec((step, columns), lambda i: (i, 0)),
        out_shape=jax.ShapeDtypeStruct((width, columns), jnp.bfloat16),
    )(hidden, grad)


def from_all(row):
    count = lax.axis_size(every_axis)
    return lax.all_to_all(
        jnp.broadcast_to(row[None, :], (count, row.shape[0])), every_axis, 0, 0, tiled=True
    )


def admitted(packed, sampled_ids, column_start):
    words = packed.shape[1]
    columns = words * 16
    word_of = jnp.arange(columns, dtype=jnp.int32) // 16
    bit_of = jnp.arange(columns, dtype=jnp.int32) % 16
    here = word_of[None, :] == jnp.arange(words, dtype=jnp.int32)[:, None]
    low_pick = (here & (bit_of < 8)[None, :]).astype(jnp.bfloat16)
    high_pick = (here & (bit_of >= 8)[None, :]).astype(jnp.bfloat16)
    low = (packed & 255).astype(jnp.bfloat16)
    high = (packed >> 8).astype(jnp.bfloat16)
    byte = jnp.dot(
        jnp.concatenate([low, high], axis=1),
        jnp.concatenate([low_pick, high_pick], axis=0),
        preferred_element_type=jnp.float32,
    ).astype(jnp.int32)
    bit = jnp.right_shift(byte, (bit_of % 8)[None, :]) & 1
    chosen = (column_start + jnp.arange(columns, dtype=jnp.int32))[None, :] == sampled_ids[:, None]
    return ((bit == 1) | chosen, chosen)


def per_device(
    teacher_hidden, teacher_head, student_hidden, student_head, grammar_bits, sampled_ids
):
    x = lax.axis_index("x")
    core = lax.axis_index("c")
    z = lax.axis_index("z")
    column_block = lax.axis_index(every_axis)
    token_total, width = student_hidden.shape
    columns = student_head.shape[1]
    rows = token_total // 2

    def teacher_block(step):
        weights = lax.dynamic_slice_in_dim(teacher_head, (x + step) % 4 * columns, columns, 1)
        return row_major(
            jnp.dot(teacher_hidden, weights, preferred_element_type=jnp.float32)
        )

    far = teacher_block(2).astype(wire)
    far = shift(far, x=2)
    after = teacher_block(1).astype(wire)
    after = shift(after, x=1)
    before = teacher_block(3).astype(wire)
    before = shift(before, x=3)
    own = lax.optimization_barrier(teacher_block(0))
    student_logit = row_major(
        jnp.dot(student_hidden, student_head, preferred_element_type=jnp.float32)
    )
    student_top = jnp.max(student_logit, axis=1)
    student_sum = jnp.sum(jnp.exp(student_logit - student_top[:, None]), axis=1)
    student_lse = student_top + jnp.log(student_sum)
    packed = lax.all_to_all(grammar_bits, "x", split_axis=1, concat_axis=0, tiled=True)
    allowed, chosen = admitted(packed, sampled_ids, column_block * columns)

    teacher_logit = row_major(own + wide(far) + (wide(after) + wide(before)))
    masked = jnp.where(allowed, teacher_logit, -1e30)
    teacher_top = jnp.max(masked, axis=1)
    teacher_sum = jnp.sum(
        jnp.where(allowed, jnp.exp(masked - teacher_top[:, None]), 0.0), axis=1
    )
    teacher_lse = jnp.where(
        teacher_sum > 0.0, teacher_top + jnp.log(jnp.maximum(teacher_sum, 1.0)), -1e30
    )
    block_at = [(z + step) % 4 for step in range(4)]
    early = jnp.stack(block_at + [core, 1 - core] + [core] * 122).astype(jnp.float32)
    every = from_all(jnp.concatenate([teacher_lse, student_lse, early]))[:, : 2 * token_total]
    top = jnp.max(every, axis=0)
    lse = top + jnp.log(jnp.sum(jnp.exp(every - top[None, :]), axis=0))
    teacher_log = teacher_logit - lse[:token_total, None]
    student_log = student_logit - lse[token_total:, None]

    teacher_prob = jnp.where(allowed, jnp.exp(teacher_log), 0.0).astype(jnp.bfloat16)
    prob_wide = wide(teacher_prob)
    logit_grad = row_major(
        (
            (1.0 - sample_weight) * jnp.exp(student_log)
            - prob_wide
            + sample_weight * wide(chosen)
        ).astype(jnp.bfloat16)
    )

    by_core = logit_grad.reshape(16, 2, 16, columns)

    def hidden_rows(which):
        part = lax.dynamic_index_in_dim(by_core, which, 1, False).reshape(rows, columns)
        return hidden_scale * lax.dot_general(
            part, student_head, (((1,), (1,)), ((), ())), preferred_element_type=jnp.float32
        )

    other = hidden_rows(1 - core).astype(wire)
    sent = shift(other, c=1).reshape(4, 64, width)
    mine = lax.optimization_barrier(hidden_rows(core)).reshape(4, 64, width)

    def block(step):
        index = block_at[step]
        return lax.dynamic_index_in_dim(mine, index, 0, False) + wide(
            lax.dynamic_index_in_dim(sent, index, 0, False)
        )

    up = shift(block(1).astype(wire), z=1)
    down = shift(block(3).astype(wire), z=3)
    across = shift(block(2).astype(wire), z=2)
    mine = block(0) + (wide(up) + wide(down)) + wide(across)

    head_grad = head_product(student_hidden, logit_grad)
    gap = teacher_log - student_log
    loss_part = jnp.sum(prob_wide * gap) - sample_weight * jnp.sum(jnp.where(chosen, gap, 0.0))
    losses = from_all(jnp.broadcast_to(loss_part, (128,)))
    distill_loss = jnp.sum(losses[:, 0]) / token_total

    last = lax.all_to_all(mine.astype(wire).reshape(16, 4, width), ("y", "x"), 0, 0, tiled=True)
    hidden_grad = jnp.sum(wide(last), axis=0) * (1.0 / hidden_scale)
    return (distill_loss, head_grad, hidden_grad)


def solution(mesh):
    split = Mesh(mesh.devices.reshape(4, 4, 2, 4), every_axis)
    vocab = ("z", "y", "c")
    placed = (
        P(None, "x"),
        P("x", vocab),
        P(),
        P(None, every_axis),
        P("x", vocab),
        P(),
    )
    return jax.shard_map(
        per_device,
        mesh=split,
        in_specs=placed,
        out_specs=(P(), P(None, every_axis), P(every_axis, None)),
        check_vma=False,
    )
```

profile of v0, /device:TPU:1, one launch (start us, length us, event | category | flops | bytes accessed | tf_op | source)
XLA Modules:
  0.0 131.5 jit_solution(4191465173916129346)
XLA Ops:
  0.6 0.0 copy-start
  0.6 5.0 %all-to-all-start = ((s32[128,4,40]{0,2,1:T(8,128)}), s32[128,4,40]{0,2,1:T(8,128)S(1)}, u32[]{:S(2)}, u32[]{:S(2)}) async-start(s32[128,4,40]{0,2,1:T(8,128)} %bitcast.70), calls=%async_computation | async-start | bytes 163840 | tf_op jit(solution)/shard_map/all_to_all | solution.py:120
  5.6 0.0 copy-done
  5.6 4.4 %fusion.30 = f16[512,640]{1,0:T(8,128)(2,1)} fusion(bf16[512,2048]{1,0:T(8,128)(2,1)S(1)} %copy-done, bf16[2048,2560]{1,0:T(8,128)(2,1)} %param.7, s32[]{:T(128)S(6)} %select_n.134), kind=kOutput, calls=%fused_computation.26 | convolution fusion | flops 1342504960 | bytes 5373956 | tf_op jit(solution)/shard_map/dot_general | solution.py:104
  10.0 3.0 %collective-permute-start = (f16[512,640]{1,0:T(8,128)(2,1)}, f16[512,640]{1,0:T(8,128)(2,1)}, u32[]{:S(2)}, u32[]{:S(2)}) collective-permute-start(f16[512,640]{1,0:T(8,128)(2,1)} %fusion.30), channel_id=1, source_target_pairs={{0,2},{1,3},{2,0},{3,1},{4,6},{5,7},{6,4},{7,5},{8,10},{9,11},{10,... | collective-permute-start | bytes 1966088 | tf_op jit(solution)/shard_map/ppermute | solution.py:27
  13.0 4.4 %fusion.24 = f16[512,640]{1,0:T(8,128)(2,1)} fusion(bf16[512,2048]{1,0:T(8,128)(2,1)S(1)} %copy-done, bf16[2048,2560]{1,0:T(8,128)(2,1)} %param.7, s32[]{:T(128)S(6)} %select_n.138), kind=kOutput, calls=%fused_computation.24 | convolution fusion | flops 1342504960 | bytes 5373956 | tf_op jit(solution)/shard_map/dot_general | solution.py:104
  17.4 0.8 collective-permute-start.2
  18.2 4.4 %fusion.27 = f16[512,640]{1,0:T(8,128)(2,1)} fusion(bf16[512,2048]{1,0:T(8,128)(2,1)S(1)} %copy-done, bf16[2048,2560]{1,0:T(8,128)(2,1)} %param.7, s32[]{:T(128)S(6)} %select_n.136), kind=kOutput, calls=%fused_computation.25 | convolution fusion | flops 1342504960 | bytes 5373956 | tf_op jit(solution)/shard_map/dot_general | solution.py:104
  22.6 0.6 collective-permute-start.1
  23.2 0.6 fusion.60
  23.8 4.7 %fusion.12 = f32[512,640]{1,0:T(8,128)} fusion(bf16[512,2048]{1,0:T(8,128)(2,1)S(1)} %copy-done, bf16[2048,2560]{1,0:T(8,128)(2,1)} %param.7, s32[]{:T(128)S(6)} %select_n.132), kind=kOutput, calls=%fused_computation.20 | convolution fusion | flops 1342177280 | bytes 6029316 | tf_op jit(solution)/shard_map/dot_general | solution.py:104
  28.5 0.0 copy-done.5
  28.6 5.4 %fusion.70 = (f32[512]{0:T(512)S(1)}, f32[512,640]{1,0:T(8,128)S(1)}) fusion(bf16[512,3584]{1,0:T(8,128)(2,1)S(1)} %copy-done.5, bf16[3584,640]{1,0:T(8,128)(2,1)} %param.9), kind=kOutput, calls=%fused_computation.99 | convolution fusion | flops 2349137408 | bytes 9570304 | tf_op jit(solution)/shard_map/dot_general | solution.py:115
  33.9 0.3 exponential_reduce_fusion
  34.3 0.0 copy-done.8
  34.4 0.2 stack.20
  34.6 0.5 convert_element_type.119
  35.2 0.6 add_select_fusion
  35.8 0.0 all-to-all-done
  35.8 0.0 collective-permute-done
  35.8 5.9 %collective-permute-done.2 = f16[512,640]{1,0:T(8,128)(2,1)} collective-permute-done((f16[512,640]{1,0:T(8,128)(2,1)}, f16[512,640]{1,0:T(8,128)(2,1)}, u32[]{:S(2)}, u32[]{:S(2)}) %collective-permute-start.2) | collective-permute-done | bytes 655392 | tf_op jit(solution)/shard_map/ppermute | solution.py:27
  41.8 0.0 collective-permute-done.1
  41.8 2.9 %fusion.39 = (f32[512]{0:T(512)S(1)}, f32[512,640]{1,0:T(8,128)S(1)}, pred[512,640]{1,0:T(8,128)(4,1)S(1)}) fusion(f16[512,640]{1,0:T(8,128)(2,1)} %collective-permute-done.2, f16[512,640]{1,0:T(8,128)(2,1)} %collective-permute-done.1, f32[512,640]{1,0:T(8,128)} %fusion.12, f16[512,640]{1,0:T(8,128)(2,1)} %collective-permute-done, s32[512]{0:T(512)} %param.11, ...), kind=kOutput, calls=%fused_computation.44 | convolution fusion | flops 57230848 | bytes 5057536 | tf_op jit(solution)/shard_map/dot_general | solution.py:80
  44.7 0.0 copy-start.3
  44.7 0.0 copy-start.6
  44.7 1.0 copy-done.3
  45.8 0.5 select_reduce_fusion
  46.3 0.0 copy-done.6
  46.3 0.0 copy-done.10
  46.3 1.1 broadcast_in_dim.18
  47.5 11.9 %all-to-all-start.1 = ((f32[128,1,1152]{2,1,0:T(1,128)}), f32[128,1,1152]{2,1,0:T(1,128)}, u32[]{:S(2)}, u32[]{:S(2)}) async-start(f32[128,1,1152]{2,1,0:T(1,128)} %broadcast_in_dim.18), calls=%async_computation.1 | async-start | bytes 1179648 | tf_op jit(solution)/shard_map/all_to_all | solution.py:65
  59.4 14.3 %all-to-all-done.1 = f32[128,1,1152]{2,1,0:T(1,128)} async-done(((f32[128,1,1152]{2,1,0:T(1,128)}), f32[128,1,1152]{2,1,0:T(1,128)}, u32[]{:S(2)}, u32[]{:S(2)}) %all-to-all-start.1) | async-done | bytes 589856 | tf_op jit(solution)/shard_map/all_to_all | solution.py:65
  73.7 1.2 copy.24
  75.0 0.1 exponential_reduce_fusion.1
  75.1 0.0 copy-done.9
  75.1 0.1 copy-done.4
  75.2 0.0 copy-done.7
  75.2 1.8 %fusion.36 = (f32[]{:T(128)}, f32[]{:T(128)}, bf16[512,640]{1,0:T(8,128)(2,1)S(1)}) fusion(s32[640]{0:T(1024)S(1)} %get-tuple-element.27, s32[512]{0:T(512)S(1)} %copy-done.9, f32[512,640]{1,0:T(8,128)S(1)} %get-tuple-element.20, f32[512]{0:T(512)S(1)} %get-tuple-element.16, f32[512,640]{1,0:T(8,128)S(1)} %copy-done.4, f32[512]{0:T(512)S(1)} %get-tuple-element.15, ...), kind=kLoop, calls=%fused_computation.30 | loop fusion | flops 5242878 | bytes 3613192 | tf_op jit(solution)/shard_map/reduce_sum | solution.py:175
  77.0 0.1 constant_dynamic-slice_fusion
  77.1 5.3 %fusion = f16[256,3584]{1,0:T(8,128)(2,1)} fusion(bf16[256,640]{1,0:T(8,128)(2,1)S(1)} %bitcast.68, bf16[3584,640]{1,0:T(8,128)(2,1)} %param.9), kind=kOutput, calls=%fused_computation.2 | convolution fusion | flops 1176240128 | bytes 6750208 | tf_op jit(solution)/shard_map/dot_general | solution.py:154
  82.4 0.0 copy-done.2
  82.4 0.3 collective-permute-start.3
  82.8 3.9 %convolution_multiply_fusion.1 = f32[256,3584]{1,0:T(8,128)S(1)} fusion(bf16[256,640]{1,0:T(8,128)(2,1)S(1)} %bitcast.67, bf16[3584,640]{1,0:T(8,128)(2,1)} %param.9), kind=kOutput, calls=%fused_computation.1 | convolution fusion | flops 1175322624 | bytes 8585216 | tf_op jit(solution)/shard_map/dot_general | solution.py:154
  86.7 0.0 copy-start.1
  86.7 0.0 collective-permute-done.3
  86.7 2.7 %fusion.40 = (f16[64,3584]{1,0:T(8,128)(2,1)S(1)}, f16[64,3584]{1,0:T(8,128)(2,1)S(1)}, f16[64,3584]{1,0:T(8,128)(2,1)S(1)}) fusion(f32[4,64,3584]{2,1,0:T(8,128)S(1)} %bitcast.62, s32[]{:T(128)S(6)} %select_n.151, f16[4,64,3584]{2,1,0:T(8,128)(2,1)} %bitcast.18, s32[]{:T(128)S(6)} %select_n.153, s32[]{:T(128)S(6)} %select_n.152), kind=kLoop, calls=%fused_computation.48 | loop fusion | flops 2064384 | bytes 5505036 | tf_op jit(solution)/shard_map/convert_element_type | solution.py:168
  89.4 0.0 copy-done.1
  89.4 0.6 collective-permute-start.4
  90.0 1.3 collective-permute-start.6
  91.3 1.5 %collective-permute-start.5 = (f16[64,3584]{1,0:T(8,128)(2,1)S(1)}, f16[64,3584]{1,0:T(8,128)(2,1)}, u32[]{:S(2)}, u32[]{:S(2)}) collective-permute-start(f16[64,3584]{1,0:T(8,128)(2,1)S(1)} %get-tuple-element.9), channel_id=1, source_target_pairs={{0,96},{1,97},{2,98},{3,99},{4,100},{5,101},{6,102},{7,103},{8,104... | collective-permute-start | bytes 1376264 | tf_op jit(solution)/shard_map/ppermute | solution.py:27
  94.1 0.7 broadcast_in_dim_broadcast_in_dim_broadcast_in_dim.3
  94.7 5.4 %all-to-all-start.2 = ((f32[128,1,128]{2,1,0:T(1,128)}), f32[128,1,128]{2,1,0:T(1,128)S(1)}, u32[]{:S(2)}, u32[]{:S(2)}) async-start(f32[128,1,128]{2,1,0:T(1,128)} %broadcast_in_dim_broadcast_in_dim_broadcast_in_dim.3), calls=%async_computation.2 | async-start | bytes 131072 | tf_op jit(solution)/shard_map/all_to_all | solution.py:65
  100.1 13.1 %collective-permute-done.4 = f16[64,3584]{1,0:T(8,128)(2,1)} collective-permute-done((f16[64,3584]{1,0:T(8,128)(2,1)S(1)}, f16[64,3584]{1,0:T(8,128)(2,1)}, u32[]{:S(2)}, u32[]{:S(2)}) %collective-permute-start.4) | collective-permute-done | bytes 458784 | tf_op jit(solution)/shard_map/ppermute | solution.py:27
  113.2 0.0 collective-permute-done.6
  113.2 0.3 collective-permute-done.5
  113.5 2.0 %fusion.38 = f16[64,3584]{1,0:T(8,128)(2,1)S(1)} fusion(f16[64,3584]{1,0:T(8,128)(2,1)} %collective-permute-done.6, f16[64,3584]{1,0:T(8,128)(2,1)} %collective-permute-done.5, f16[64,3584]{1,0:T(8,128)(2,1)} %collective-permute-done.4, f32[4,64,3584]{2,1,0:T(8,128)} %bitcast.63, s32[]{:T(128)S(6)} %select_n.149, f16[4,64,3584]{2,1,0:T(8,128)(2,1)} %bitcast.18), kind=kLoop, calls=%fused_computation.38 | loop fusion | flops 2064384 | bytes 3211268 | tf_op jit(solution)/shard_map/convert_element_type | solution.py:179
  115.5 0.9 reshape.108
  116.4 0.0 all-to-all-done.2
  116.4 3.6 %all-to-all-start.3 = ((f16[16,4,3584]{2,1,0:T(4,128)(2,1)}), f16[16,4,3584]{2,1,0:T(4,128)(2,1)S(1)}, u32[]{:S(2)}, u32[]{:S(2)}) async-start(f16[16,4,3584]{2,1,0:T(4,128)(2,1)} %reshape.108), calls=%async_computation.3 | async-start | bytes 917504 | tf_op jit(solution)/shard_map/all_to_all | solution.py:179
  120.0 6.8 %shard_map.85 = bf16[3584,640]{1,0:T(8,128)(2,1)} custom-call(bf16[512,3584]{1,0:T(8,128)(2,1)} %hidden_ref.1, bf16[512,640]{1,0:T(8,128)(2,1)} %copy-done.2), custom_call_target="tpu_custom_call" | custom-call | tf_op jit(solution)/shard_map/pallas_call | solution.py:51
  126.8 0.6 slice_reduce_fusion.1
  128.1 1.4 %all-to-all-done.3 = f16[16,4,3584]{2,1,0:T(4,128)(2,1)S(1)} async-done(((f16[16,4,3584]{2,1,0:T(4,128)(2,1)}), f16[16,4,3584]{2,1,0:T(4,128)(2,1)S(1)}, u32[]{:S(2)}, u32[]{:S(2)}) %all-to-all-start.3) | async-done | bytes 458784 | tf_op jit(solution)/shard_map/all_to_all | solution.py:179
  129.5 0.2 convert_reduce_fusion
  129.7 0.6 broadcast_multiply_fusion
  (17 shorter events, 0.2 us)
Async XLA Ops:
  0.6 5.0 %copy-start = (bf16[512,2048]{1,0:T(8,128)(2,1)S(1)}, bf16[512,2048]{1,0:T(8,128)(2,1)}, u32[]{:S(2)}) copy-start(bf16[512,2048]{1,0:T(8,128)(2,1)} %param.6) | copy-start | bytes 6291460
  0.6 35.1 %all-to-all-start = ((s32[128,4,40]{0,2,1:T(8,128)}), s32[128,4,40]{0,2,1:T(8,128)S(1)}, u32[]{:S(2)}, u32[]{:S(2)}) async-start(s32[128,4,40]{0,2,1:T(8,128)} %bitcast.70), calls=%async_computation | async-start | bytes 163840 | tf_op jit(solution)/shard_map/all_to_all | solution.py:120
  10.0 25.8 %collective-permute-start = (f16[512,640]{1,0:T(8,128)(2,1)}, f16[512,640]{1,0:T(8,128)(2,1)}, u32[]{:S(2)}, u32[]{:S(2)}) collective-permute-start(f16[512,640]{1,0:T(8,128)(2,1)} %fusion.30), channel_id=1, source_target_pairs={{0,2},{1,3},{2,0},{3,1},{4,6},{5,7},{6,4},{7,5},{8,10},{9,11},{10,... | collective-permute-start | bytes 1966088 | tf_op jit(solution)/shard_map/ppermute | solution.py:27
  17.4 24.4 %collective-permute-start.2 = (f16[512,640]{1,0:T(8,128)(2,1)}, f16[512,640]{1,0:T(8,128)(2,1)}, u32[]{:S(2)}, u32[]{:S(2)}) collective-permute-start(f16[512,640]{1,0:T(8,128)(2,1)} %fusion.24), channel_id=1, source_target_pairs={{0,3},{1,0},{2,1},{3,2},{4,7},{5,4},{6,5},{7,6},{8,11},{9,8},{10,9... | collective-permute-start | bytes 1966088 | tf_op jit(solution)/shard_map/ppermute | solution.py:27
  22.6 19.2 %collective-permute-start.1 = (f16[512,640]{1,0:T(8,128)(2,1)}, f16[512,640]{1,0:T(8,128)(2,1)}, u32[]{:S(2)}, u32[]{:S(2)}) collective-permute-start(f16[512,640]{1,0:T(8,128)(2,1)} %fusion.27), channel_id=1, source_target_pairs={{0,1},{1,2},{2,3},{3,0},{4,5},{5,6},{6,7},{7,4},{8,9},{9,10},{10,1... | collective-permute-start | bytes 1966088 | tf_op jit(solution)/shard_map/ppermute | solution.py:27
  23.8 4.7 %copy-start.5 = (bf16[512,3584]{1,0:T(8,128)(2,1)S(1)}, bf16[512,3584]{1,0:T(8,128)(2,1)}, u32[]{:S(2)}) copy-start(bf16[512,3584]{1,0:T(8,128)(2,1)} %hidden_ref.1) | copy-start | bytes 11010052
  28.5 5.7 %copy-start.8 = (pred[640]{0:T(1024)(128)(4,1)S(1)}, pred[640]{0:T(1024)(128)(4,1)}, u32[]{:S(2)}) copy-start(pred[640]{0:T(1024)(128)(4,1)} %get-tuple-element.23) | copy-start | bytes 1924
  41.8 4.5 %copy-start.10 = (f32[128]{0:T(128)S(1)}, f32[128]{0:T(128)}, u32[]{:S(2)}) copy-start(f32[128]{0:T(128)} %convert_element_type.119) | copy-start | bytes 1540
  44.7 1.1 copy-start.3
  44.7 1.6 %copy-start.6 = (pred[512,640]{1,0:T(8,128)(4,1)}, pred[512,640]{1,0:T(8,128)(4,1)S(1)}, u32[]{:S(2)}) copy-start(pred[512,640]{1,0:T(8,128)(4,1)S(1)} %get-tuple-element.21) | copy-start | bytes 983044
  47.5 27.6 %copy-start.9 = (s32[512]{0:T(512)S(1)}, s32[512]{0:T(512)}, u32[]{:S(2)}) copy-start(s32[512]{0:T(512)} %param.11) | copy-start | bytes 6148
  47.5 26.2 %all-to-all-start.1 = ((f32[128,1,1152]{2,1,0:T(1,128)}), f32[128,1,1152]{2,1,0:T(1,128)}, u32[]{:S(2)}, u32[]{:S(2)}) async-start(f32[128,1,1152]{2,1,0:T(1,128)} %broadcast_in_dim.18), calls=%async_computation.1 | async-start | bytes 1179648 | tf_op jit(solution)/shard_map/all_to_all | solution.py:65
  73.7 1.5 %copy-start.4 = (f32[512,640]{1,0:T(8,128)S(1)}, f32[512,640]{1,0:T(8,128)}, u32[]{:S(2)}) copy-start(f32[512,640]{1,0:T(8,128)} %copy-done.3) | copy-start | bytes 3932164
  73.7 1.5 %copy-start.7 = (pred[512,640]{1,0:T(8,128)(4,1)S(1)}, pred[512,640]{1,0:T(8,128)(4,1)}, u32[]{:S(2)}) copy-start(pred[512,640]{1,0:T(8,128)(4,1)} %copy-done.6) | copy-start | bytes 983044
  77.0 5.4 %copy-start.2 = (bf16[512,640]{1,0:T(8,128)(2,1)}, bf16[512,640]{1,0:T(8,128)(2,1)S(1)}, u32[]{:S(2)}) copy-start(bf16[512,640]{1,0:T(8,128)(2,1)S(1)} %get-tuple-element.10.grad_ref) | copy-start | bytes 1966084
  82.4 4.3 %collective-permute-start.3 = (f16[256,3584]{1,0:T(8,128)(2,1)}, f16[256,3584]{1,0:T(8,128)(2,1)}, u32[]{:S(2)}, u32[]{:S(2)}) collective-permute-start(f16[256,3584]{1,0:T(8,128)(2,1)} %fusion), channel_id=1, source_target_pairs={{0,4},{1,5},{2,6},{3,7},{4,0},{5,1},{6,2},{7,3},{8,12},{9,13},{10,... | collective-permute-start | bytes 5505032 | tf_op jit(solution)/shard_map/ppermute | solution.py:27
  86.7 2.7 %copy-start.1 = (f32[256,3584]{1,0:T(8,128)}, f32[256,3584]{1,0:T(8,128)S(1)}, u32[]{:S(2)}) copy-start(f32[256,3584]{1,0:T(8,128)S(1)} %convolution_multiply_fusion.1) | copy-start | bytes 11010052
  89.4 23.8 %collective-permute-start.4 = (f16[64,3584]{1,0:T(8,128)(2,1)S(1)}, f16[64,3584]{1,0:T(8,128)(2,1)}, u32[]{:S(2)}, u32[]{:S(2)}) collective-permute-start(f16[64,3584]{1,0:T(8,128)(2,1)S(1)} %get-tuple-element.7), channel_id=1, source_target_pairs={{0,32},{1,33},{2,34},{3,35},{4,36},{5,37},{6,38},{7,39},{8,40},{9,... | collective-permute-start | bytes 1376264 | tf_op jit(solution)/shard_map/ppermute | solution.py:27
  90.0 23.2 %collective-permute-start.6 = (f16[64,3584]{1,0:T(8,128)(2,1)S(1)}, f16[64,3584]{1,0:T(8,128)(2,1)}, u32[]{:S(2)}, u32[]{:S(2)}) collective-permute-start(f16[64,3584]{1,0:T(8,128)(2,1)S(1)} %get-tuple-element.8), channel_id=1, source_target_pairs={{0,64},{1,65},{2,66},{3,67},{4,68},{5,69},{6,70},{7,71},{8,72},{9,... | collective-permute-start | bytes 1376264 | tf_op jit(solution)/shard_map/ppermute | solution.py:27
  91.3 22.3 %collective-permute-start.5 = (f16[64,3584]{1,0:T(8,128)(2,1)S(1)}, f16[64,3584]{1,0:T(8,128)(2,1)}, u32[]{:S(2)}, u32[]{:S(2)}) collective-permute-start(f16[64,3584]{1,0:T(8,128)(2,1)S(1)} %get-tuple-element.9), channel_id=1, source_target_pairs={{0,96},{1,97},{2,98},{3,99},{4,100},{5,101},{6,102},{7,103},{8,104... | collective-permute-start | bytes 1376264 | tf_op jit(solution)/shard_map/ppermute | solution.py:27
  94.7 21.7 %all-to-all-start.2 = ((f32[128,1,128]{2,1,0:T(1,128)}), f32[128,1,128]{2,1,0:T(1,128)S(1)}, u32[]{:S(2)}, u32[]{:S(2)}) async-start(f32[128,1,128]{2,1,0:T(1,128)} %broadcast_in_dim_broadcast_in_dim_broadcast_in_dim.3), calls=%async_computation.2 | async-start | bytes 131072 | tf_op jit(solution)/shard_map/all_to_all | solution.py:65
  116.4 13.1 %all-to-all-start.3 = ((f16[16,4,3584]{2,1,0:T(4,128)(2,1)}), f16[16,4,3584]{2,1,0:T(4,128)(2,1)S(1)}, u32[]{:S(2)}, u32[]{:S(2)}) async-start(f16[16,4,3584]{2,1,0:T(4,128)(2,1)} %reshape.108), calls=%async_computation.3 | async-start | bytes 917504 | tf_op jit(solution)/shard_map/all_to_all | solution.py:179
where the time goes:
time: 133 us; the launch traced here: 131 us
  matrix products  35.4 us (27%)
  waiting for transfers between devices  35.1 us (26%)
  starting transfers between devices  34 us (26%)
  other arithmetic  10.7 us (8%)
  Pallas kernels  6.83 us (5%)
  local copies, waits for them, and re-layouts  5.44 us (4%)
  between operations  3.97 us (3%)
    ppermute x7, waiting for transfers between devices, shift(): return lax.ppermute(value, every_axis, pairs)  19.4 us
    dot_general x4, matrix products, teacher_block(): jnp.dot(teacher_hidden, weights, preferred_element_type=jnp.float32)  17.8 us
    all_to_all x2, starting transfers between devices, from_all(): lax.all_to_all(jnp.broadcast_to(row[None, :], (count, row.shape[0])), eve...  17.3 us
    all_to_all x2, waiting for transfers between devices, from_all(): lax.all_to_all(jnp.broadcast_to(row[None, :], (count, row.shape[0])), eve...  14.3 us
    dot_general x2, matrix products, hidden_rows(): lax.dot_general(part, student_head, (((1,), (1,)), ((), ())), preferred_e...  9.26 us
    ppermute x7, starting transfers between devices, shift(): return lax.ppermute(value, every_axis, pairs)  8.22 us
    pallas_call x1, Pallas kernels, head_product(): pl.pallas_call(head_kernel, grid=(4,), in_specs=[pl.BlockSpec((tokens, st...  6.83 us
    dot_general x1, matrix products, per_device(): jnp.dot(student_hidden, student_head, preferred_element_type=jnp.float32)  5.39 us
  transfers between devices with their start and end apart: 11, of which 5 were waited for; matrix products, arithmetic and copies ran while one was open for 26% of the time, Pallas kernels for 5%

commit v1 on v0

--- a/solution.py
+++ b/solution.py
@@ -25,6 +25,56 @@
         for h in range(4)
     ]
     return lax.ppermute(value, every_axis, pairs)
+
+
+def swap(value, z=0, y=0, c=0, x=0):
+    pairs = [
+        (device_of(k, j, i, h), device_of(k ^ z, j ^ y, i ^ c, h ^ x))
+        for k in range(4)
+        for j in range(4)
+        for i in range(2)
+        for h in range(4)
+    ]
+    return lax.ppermute(value, every_axis, pairs)
+
+
+def core_shift(value, step):
+    pairs = [
+        (
+            device_of(k, j, i, h),
+            device_of(k, j + step, i, h) if i == 0 else device_of(k + step, j, i, h),
+        )
+        for k in range(4)
+        for j in range(4)
+        for i in range(2)
+        for h in range(4)
+    ]
+    return lax.ppermute(value, every_axis, pairs)
+
+
+plane_groups = [
+    [device_of(k, j, 0, h) for k in range(4) for h in range(4)] for j in range(4)
+] + [[device_of(k, j, 1, h) for j in range(4) for h in range(4)] for k in range(4)]
+
+
+def merged(parts):
+    scores = [part[:8] for part in parts]
+    terms = [part[8:] for part in parts]
+    top = scores[0]
+    for score in scores[1:]:
+        top = jnp.maximum(top, score)
+    shares = [jnp.exp(score - top) for score in scores]
+    while len(shares) > 1:
+        shares = [shares[i] + shares[i + 1] for i in range(0, len(shares), 2)]
+    total = top + jnp.log(shares[0])
+    is_gap = lax.broadcasted_iota(jnp.int32, (8, 128), 0) < 4
+    weighed = [
+        jnp.where(is_gap, jnp.exp(score - total), 1.0) * term
+        for score, term in zip(scores, terms)
+    ]
+    while len(weighed) > 1:
+        weighed = [weighed[i] + weighed[i + 1] for i in range(0, len(weighed), 2)]
+    return jnp.concatenate([total, weighed[0]])
 
 
 def wide(a):
@@ -58,13 +108,6 @@
         out_specs=pl.BlockSpec((step, columns), lambda i: (i, 0)),
         out_shape=jax.ShapeDtypeStruct((width, columns), jnp.bfloat16),
     )(hidden, grad)
-
-
-def from_all(row):
-    count = lax.axis_size(every_axis)
-    return lax.all_to_all(
-        jnp.broadcast_to(row[None, :], (count, row.shape[0])), every_axis, 0, 0, tiled=True
-    )
 
 
 def admitted(packed, sampled_ids, column_start):
@@ -92,7 +135,7 @@
 ):
     x = lax.axis_index("x")
     core = lax.axis_index("c")
-    z = lax.axis_index("z")
+    place = jnp.where(core == 0, lax.axis_index("y"), lax.axis_index("z"))
     column_block = lax.axis_index(every_axis)
     token_total, width = student_hidden.shape
     columns = student_head.shape[1]
@@ -123,17 +166,25 @@
     teacher_logit = row_major(own + wide(far) + (wide(after) + wide(before)))
     masked = jnp.where(allowed, teacher_logit, -1e30)
     teacher_top = jnp.max(masked, axis=1)
-    teacher_sum = jnp.sum(
-        jnp.where(allowed, jnp.exp(masked - teacher_top[:, None]), 0.0), axis=1
-    )
-    teacher_lse = jnp.where(
-        teacher_sum > 0.0, teacher_top + jnp.log(jnp.maximum(teacher_sum, 1.0)), -1e30
-    )
-    block_at = [(z + step) % 4 for step in range(4)]
-    early = jnp.stack(block_at + [core, 1 - core] + [core] * 122).astype(jnp.float32)
-    every = from_all(jnp.concatenate([teacher_lse, student_lse, early]))[:, : 2 * token_total]
-    top = jnp.max(every, axis=0)
-    lse = top + jnp.log(jnp.sum(jnp.exp(every - top[None, :]), axis=0))
+    weight = jnp.where(allowed, jnp.exp(masked - teacher_top[:, None]), 0.0)
+    gap = teacher_logit - student_logit
+    teacher_sum = jnp.maximum(jnp.sum(weight, axis=1), 1e-30)
+    teacher_lse = jnp.maximum(teacher_top + jnp.log(teacher_sum), -1e30)
+    gap_mean = jnp.sum(weight * gap, axis=1) / teacher_sum
+    picked = jnp.sum(jnp.where(chosen, gap, 0.0), axis=1)
+    stats = jnp.concatenate([teacher_lse, student_lse, gap_mean, picked]).reshape(16, 128)
+    stats = merged([stats, swap(stats, c=1)])
+    for axis in ("x", "y", "z"):
+        far_stats = swap(stats, **{axis: 2})
+        near_stats = swap(stats, **{axis: 1})
+        next_stats = swap(stats, **{axis: 3})
+        stats = merged([stats, far_stats, near_stats, next_stats])
+    lse = stats[:8].reshape(2 * token_total)
+    apart = stats[4:8] - stats[:4]
+    distill_loss = (
+        jnp.sum(stats[8:12] + (1.0 - sample_weight) * apart - sample_weight * stats[12:])
+        / token_total
+    )
     teacher_log = teacher_logit - lse[:token_total, None]
     student_log = student_logit - lse[token_total:, None]
 
@@ -150,7 +201,8 @@
     by_core = logit_grad.reshape(16, 2, 16, columns)
 
     def hidden_rows(which):
-        part = lax.dynamic_index_in_dim(by_core, which, 1, False).reshape(rows, columns)
+        part = lax.dynamic_index_in_dim(by_core, which, 1, False).reshape(4, 4, 16, columns)
+        part = jnp.where(which == 0, part.swapaxes(0, 1), part).reshape(rows, columns)
         return hidden_scale * lax.dot_general(
             part, student_head, (((1,), (1,)), ((), ())), preferred_element_type=jnp.float32
         )
@@ -160,23 +212,25 @@
     mine = lax.optimization_barrier(hidden_rows(core)).reshape(4, 64, width)
 
     def block(step):
-        index = block_at[step]
+        index = (place + step) % 4
         return lax.dynamic_index_in_dim(mine, index, 0, False) + wide(
             lax.dynamic_index_in_dim(sent, index, 0, False)
         )
 
-    up = shift(block(1).astype(wire), z=1)
-    down = shift(block(3).astype(wire), z=3)
-    across = shift(block(2).astype(wire), z=2)
+    up = core_shift(block(1).astype(wire), 1)
+    down = core_shift(block(3).astype(wire), 3)
+    across = core_shift(block(2).astype(wire), 2)
     mine = block(0) + (wide(up) + wide(down)) + wide(across)
 
     head_grad = head_product(student_hidden, logit_grad)
-    gap = teacher_log - student_log
-    loss_part = jnp.sum(prob_wide * gap) - sample_weight * jnp.sum(jnp.where(chosen, gap, 0.0))
-    losses = from_all(jnp.broadcast_to(loss_part, (128,)))
-    distill_loss = jnp.sum(losses[:, 0]) / token_total
-
-    last = lax.all_to_all(mine.astype(wire).reshape(16, 4, width), ("y", "x"), 0, 0, tiled=True)
+    last = lax.all_to_all(
+        mine.astype(wire).reshape(16, 4, width),
+        every_axis,
+        0,
+        0,
+        axis_index_groups=plane_groups,
+        tiled=True,
+    )
     hidden_grad = jnp.sum(wide(last), axis=0) * (1.0 / hidden_scale)
     return (distill_loss, head_grad, hidden_grad)
 

time: 133 us -> 124 us (0.932)
  waiting for transfers between devices: 35.1 us -> 27.4 us
  local copies, waits for them, and re-layouts: 5.44 us -> 1.04 us
  starting transfers between devices: 34 us -> 37.7 us
  between operations: 3.97 us -> 2.64 us
    ppermute x0 -> x13, waiting for transfers between devices: none -> 19.1 us  [the longest x3 10.2 us: core_shift(): return lax.ppermute(value, every_axis, pairs)]
    ppermute x0 -> x13, starting transfers between devices: none -> 19 us  [the longest x10 14.7 us: swap(): return lax.ppermute(value, every_axis, pairs)]
    all_to_all x3 -> x1, starting transfers between devices: 20.9 us -> 4.18 us  [per_device(): lax.all_to_all(mine.astype(wire).reshape(16, 4, width), every_axis, 0, 0,...]
    all_to_all x3 -> x1, waiting for transfers between devices: 15.7 us -> 1.77 us  [per_device(): lax.all_to_all(mine.astype(wire).reshape(16, 4, width), every_axis, 0, 0,...]
    ppermute x7 -> x4, waiting for transfers between devices: 19.4 us -> 6.54 us  [shift(): return lax.ppermute(value, every_axis, pairs)]
    unnamed x23 -> x20, local copies, waits for them, and re-layouts: 2.44 us -> 0.05 us
    reduce_sum x5 -> x1, other arithmetic: 3.35 us -> 1.19 us  [per_device(): gap_mean = jnp.sum(weight * gap, axis=1) / teacher_sum]
    convert_element_type x2, other arithmetic: 3.21 us -> 4.78 us  [the longest x1 2.66 us: per_device(): up = core_shift(block(1).astype(wire), 1)]
  transfers between devices with their start and end apart: 11 -> 19, of which waited for: 5 -> 11; matrix products, arithmetic and copies ran while one was open for 26% -> 24% of each run, Pallas kernels for 5% -> 6%
where the time goes in v1:
time: 124 us; the launch traced here: 123 us
  starting transfers between devices  37.7 us (30%)
  matrix products  35.9 us (29%)
  waiting for transfers between devices  27.4 us (22%)
  other arithmetic  11 us (9%)
  Pallas kernels  6.84 us (6%)
  between operations  2.64 us (2%)
    dot_general x4, matrix products, teacher_block(): jnp.dot(teacher_hidden, weights, preferred_element_type=jnp.float32)  17.8 us
    ppermute x10, starting transfers between devices, swap(): return lax.ppermute(value, every_axis, pairs)  14.7 us
    ppermute x3, waiting for transfers between devices, core_shift(): return lax.ppermute(value, every_axis, pairs)  10.2 us
    ppermute x4, starting transfers between devices, shift(): return lax.ppermute(value, every_axis, pairs)  9.55 us
    dot_general x2, matrix products, hidden_rows(): lax.dot_general(part, student_head, (((1,), (1,)), ((), ())), preferred_e...  9.19 us
    ppermute x10, waiting for transfers between devices, swap(): return lax.ppermute(value, every_axis, pairs)  8.81 us
    pallas_call x1, Pallas kernels, head_product(): pl.pallas_call(head_kernel, grid=(4,), in_specs=[pl.BlockSpec((tokens, st...  6.84 us
    ppermute x4, waiting for transfers between devices, shift(): return lax.ppermute(value, every_axis, pairs)  6.54 us
  transfers between devices with their start and end apart: 19, of which 11 were waited for; matrix products, arithmetic and copies ran while one was open for 24% of the time, Pallas kernels for 6%

profile of v1, /device:TPU:1, one launch (start us, length us, event | category | flops | bytes accessed | tf_op | source)
XLA Modules:
  0.0 122.5 jit_solution(15091961722960881611)
XLA Ops:
  0.6 0.0 copy-start
  0.6 5.0 %all-to-all-start = ((s32[128,4,40]{0,2,1:T(8,128)}), s32[128,4,40]{0,2,1:T(8,128)S(1)}, u32[]{:S(2)}, u32[]{:S(2)}) async-start(s32[128,4,40]{0,2,1:T(8,128)} %bitcast.80), calls=%async_computation | async-start | bytes 163840 | tf_op jit(solution)/shard_map/all_to_all | solution.py:163
  5.6 4.4 %fusion.30 = f16[512,640]{1,0:T(8,128)(2,1)} fusion(bf16[512,2048]{1,0:T(8,128)(2,1)S(1)} %copy-done, bf16[2048,2560]{1,0:T(8,128)(2,1)} %param.7, s32[]{:T(128)S(6)} %select_n.190), kind=kOutput, calls=%fused_computation.24 | convolution fusion | flops 1342504960 | bytes 5373956 | tf_op jit(solution)/shard_map/dot_general | solution.py:147
  10.0 3.0 %collective-permute-start = (f16[512,640]{1,0:T(8,128)(2,1)}, f16[512,640]{1,0:T(8,128)(2,1)}, u32[]{:S(2)}, u32[]{:S(2)}) collective-permute-start(f16[512,640]{1,0:T(8,128)(2,1)} %fusion.30), channel_id=1, source_target_pairs={{0,2},{1,3},{2,0},{3,1},{4,6},{5,7},{6,4},{7,5},{8,10},{9,11},{10,... | collective-permute-start | bytes 1966088 | tf_op jit(solution)/shard_map/ppermute | solution.py:27
  13.0 4.4 %fusion.24 = f16[512,640]{1,0:T(8,128)(2,1)} fusion(bf16[512,2048]{1,0:T(8,128)(2,1)S(1)} %copy-done, bf16[2048,2560]{1,0:T(8,128)(2,1)} %param.7, s32[]{:T(128)S(6)} %select_n.194), kind=kOutput, calls=%fused_computation.22 | convolution fusion | flops 1342504960 | bytes 5373956 | tf_op jit(solution)/shard_map/dot_general | solution.py:147
  17.4 0.8 collective-permute-start.2
  18.2 4.4 %fusion.27 = f16[512,640]{1,0:T(8,128)(2,1)} fusion(bf16[512,2048]{1,0:T(8,128)(2,1)S(1)} %copy-done, bf16[2048,2560]{1,0:T(8,128)(2,1)} %param.7, s32[]{:T(128)S(6)} %select_n.192), kind=kOutput, calls=%fused_computation.23 | convolution fusion | flops 1342504960 | bytes 5373956 | tf_op jit(solution)/shard_map/dot_general | solution.py:147
  22.6 0.6 collective-permute-start.1
  23.2 0.6 fusion.60
  23.8 4.7 %fusion.12 = f32[512,640]{1,0:T(8,128)} fusion(bf16[512,2048]{1,0:T(8,128)(2,1)S(1)} %copy-done, bf16[2048,2560]{1,0:T(8,128)(2,1)} %param.7, s32[]{:T(128)S(6)} %select_n.188), kind=kOutput, calls=%fused_computation.18 | convolution fusion | flops 1342177280 | bytes 6029316 | tf_op jit(solution)/shard_map/dot_general | solution.py:147
  28.5 6.0 %fusion.80 = (f32[512]{0:T(512)}, f32[512,640]{1,0:T(8,128)S(1)}) fusion(bf16[512,3584]{1,0:T(8,128)(2,1)S(1)} %copy-done.4, bf16[3584,640]{1,0:T(8,128)(2,1)} %param.9), kind=kOutput, calls=%fused_computation.129 | convolution fusion | flops 2349137408 | bytes 9570304 | tf_op jit(solution)/shard_map/dot_general | solution.py:158
  34.6 0.6 add_select_fusion
  35.2 0.0 all-to-all-done
  35.2 0.0 collective-permute-done
  35.2 6.5 %collective-permute-done.2 = f16[512,640]{1,0:T(8,128)(2,1)} collective-permute-done((f16[512,640]{1,0:T(8,128)(2,1)}, f16[512,640]{1,0:T(8,128)(2,1)}, u32[]{:S(2)}, u32[]{:S(2)}) %collective-permute-start.2) | collective-permute-done | bytes 655392 | tf_op jit(solution)/shard_map/ppermute | solution.py:27
  41.8 0.0 collective-permute-done.1
  41.8 2.9 %fusion.39 = (f32[512]{0:T(512)S(1)}, f32[512,640]{1,0:T(8,128)S(1)}, pred[512,640]{1,0:T(8,128)(4,1)S(1)}) fusion(f16[512,640]{1,0:T(8,128)(2,1)} %collective-permute-done.2, f16[512,640]{1,0:T(8,128)(2,1)} %collective-permute-done.1, f32[512,640]{1,0:T(8,128)} %fusion.12, f16[512,640]{1,0:T(8,128)(2,1)} %collective-permute-done, s32[512]{0:T(512)S(1)} %copy-done.6, ...), kind=kOutput, calls=%fused_computation.42 | convolution fusion | flops 57230848 | bytes 5057536 | tf_op jit(solution)/shard_map/dot_general | solution.py:123
  44.7 0.0 copy-start.3
  44.7 1.2 multiply_reduce_fusion
  46.0 1.6 %collective-permute-start.3 = (f32[16,128]{1,0:T(8,128)S(1)}, f32[16,128]{1,0:T(8,128)S(1)}, u32[]{:S(2)}, u32[]{:S(2)}) collective-permute-start(f32[16,128]{1,0:T(8,128)S(1)} %pad_maximum_fusion), channel_id=1, source_target_pairs={{0,4},{1,5},{2,6},{3,7},{4,0},{5,1},{6,2},{7,3},{8,12},{9,13},{10,... | collective-permute-start | bytes 24584 | tf_op jit(solution)/shard_map/ppermute | solution.py:38
  47.6 0.8 collective-permute-done.3
  48.4 0.1 fusion.72
  48.5 2.4 %collective-permute-start.6 = (f32[16,128]{1,0:T(8,128)S(1)}, f32[16,128]{1,0:T(8,128)S(1)}, u32[]{:S(2)}, u32[]{:S(2)}) collective-permute-start(f32[16,128]{1,0:T(8,128)S(1)} %pad_maximum_fusion.1), channel_id=1, source_target_pairs={{0,3},{1,2},{2,1},{3,0},{4,7},{5,6},{6,5},{7,4},{8,11},{9,10},{10,... | collective-permute-start | bytes 24584 | tf_op jit(solution)/shard_map/ppermute | solution.py:38
  50.9 0.0 collective-permute-start.5
  50.9 1.5 %collective-permute-start.4 = (f32[16,128]{1,0:T(8,128)S(1)}, f32[16,128]{1,0:T(8,128)S(1)}, u32[]{:S(2)}, u32[]{:S(2)}) collective-permute-start(f32[16,128]{1,0:T(8,128)S(1)} %pad_maximum_fusion.1), channel_id=1, source_target_pairs={{0,2},{1,3},{2,0},{3,1},{4,6},{5,7},{6,4},{7,5},{8,10},{9,11},{10,... | collective-permute-start | bytes 24584 | tf_op jit(solution)/shard_map/ppermute | solution.py:38
  52.4 0.0 collective-permute-done.6
  52.4 1.0 collective-permute-done.5
  53.4 1.5 %collective-permute-done.4 = f32[16,128]{1,0:T(8,128)S(1)} collective-permute-done((f32[16,128]{1,0:T(8,128)S(1)}, f32[16,128]{1,0:T(8,128)S(1)}, u32[]{:S(2)}, u32[]{:S(2)}) %collective-permute-start.4) | collective-permute-done | bytes 8224 | tf_op jit(solution)/shard_map/ppermute | solution.py:38
  54.9 0.1 fusion.70
  55.0 2.8 %collective-permute-start.9 = (f32[16,128]{1,0:T(8,128)S(1)}, f32[16,128]{1,0:T(8,128)S(1)}, u32[]{:S(2)}, u32[]{:S(2)}) collective-permute-start(f32[16,128]{1,0:T(8,128)S(1)} %pad_maximum_fusion.2), channel_id=1, source_target_pairs={{0,24},{1,25},{2,26},{3,27},{4,28},{5,29},{6,30},{7,31},{8,16},{9,... | collective-permute-start | bytes 24584 | tf_op jit(solution)/shard_map/ppermute | solution.py:38
  57.8 0.0 collective-permute-start.8
  57.8 1.3 %collective-permute-start.7 = (f32[16,128]{1,0:T(8,128)S(1)}, f32[16,128]{1,0:T(8,128)S(1)}, u32[]{:S(2)}, u32[]{:S(2)}) collective-permute-start(f32[16,128]{1,0:T(8,128)S(1)} %pad_maximum_fusion.2), channel_id=1, source_target_pairs={{0,16},{1,17},{2,18},{3,19},{4,20},{5,21},{6,22},{7,23},{8,24},{9,... | collective-permute-start | bytes 24584 | tf_op jit(solution)/shard_map/ppermute | solution.py:38
  59.1 0.0 collective-permute-done.9
  59.1 1.2 collective-permute-done.8
  60.3 1.5 %collective-permute-done.7 = f32[16,128]{1,0:T(8,128)S(1)} collective-permute-done((f32[16,128]{1,0:T(8,128)S(1)}, f32[16,128]{1,0:T(8,128)S(1)}, u32[]{:S(2)}, u32[]{:S(2)}) %collective-permute-start.7) | collective-permute-done | bytes 8224 | tf_op jit(solution)/shard_map/ppermute | solution.py:38
  61.8 0.1 fusion.67
  61.9 3.8 %collective-permute-start.12 = (f32[16,128]{1,0:T(8,128)S(1)}, f32[16,128]{1,0:T(8,128)S(1)}, u32[]{:S(2)}, u32[]{:S(2)}) collective-permute-start(f32[16,128]{1,0:T(8,128)S(1)} %pad_maximum_fusion.3), channel_id=1, source_target_pairs={{0,96},{1,97},{2,98},{3,99},{4,100},{5,101},{6,102},{7,103},{8,104... | collective-permute-start | bytes 24584 | tf_op jit(solution)/shard_map/ppermute | solution.py:38
  65.7 0.0 collective-permute-start.11
  65.7 1.3 %collective-permute-start.10 = (f32[16,128]{1,0:T(8,128)S(1)}, f32[16,128]{1,0:T(8,128)S(1)}, u32[]{:S(2)}, u32[]{:S(2)}) collective-permute-start(f32[16,128]{1,0:T(8,128)S(1)} %pad_maximum_fusion.3), channel_id=1, source_target_pairs={{0,64},{1,65},{2,66},{3,67},{4,68},{5,69},{6,70},{7,71},{8,72},{9,... | collective-permute-start | bytes 24584 | tf_op jit(solution)/shard_map/ppermute | solution.py:38
  67.0 0.0 collective-permute-done.12
  67.0 1.2 collective-permute-done.11
  68.2 1.5 %collective-permute-done.10 = f32[16,128]{1,0:T(8,128)S(1)} collective-permute-done((f32[16,128]{1,0:T(8,128)S(1)}, f32[16,128]{1,0:T(8,128)S(1)}, u32[]{:S(2)}, u32[]{:S(2)}) %collective-permute-start.10) | collective-permute-done | bytes 8224 | tf_op jit(solution)/shard_map/ppermute | solution.py:38
  69.7 0.1 fusion.64
  69.8 0.6 slice_bitcast_fusion.1
  70.4 2.1 %fusion.35.grad_ref = bf16[512,640]{1,0:T(8,128)(2,1)S(1)} fusion(f32[512,640]{1,0:T(8,128)S(1)} %get-tuple-element.33, pred[512,640]{1,0:T(8,128)(4,1)} %copy-done.5, f32[512,640]{1,0:T(8,128)} %copy-done.3, f32[512]{0:T(512)S(1)} %get-tuple-element.26, f32[512]{0:T(512)S(1)} %get-tuple-element.24, s32[640]{0:T(1024)S(1)} %get-tuple-element.39, ...), kind=kLoop, calls=%fused_computation.27 | loop fusion | flops 3604480 | bytes 3613184 | tf_op jit(solution)/shard_map/convert_element_type | solution.py:198
  72.5 0.1 constant_dynamic-slice_fusion
  72.7 5.3 %fusion = f16[256,3584]{1,0:T(8,128)(2,1)} fusion(bf16[256,640]{1,0:T(8,128)(2,1)S(1)} %bitcast.79, bf16[3584,640]{1,0:T(8,128)(2,1)} %param.9), kind=kOutput, calls=%fused_computation.2 | convolution fusion | flops 1176240128 | bytes 6750208 | tf_op jit(solution)/shard_map/dot_general | solution.py:206
  77.9 5.0 %collective-permute-start.13 = (f16[256,3584]{1,0:T(8,128)(2,1)}, f16[256,3584]{1,0:T(8,128)(2,1)}, u32[]{:S(2)}, u32[]{:S(2)}) collective-permute-start(f16[256,3584]{1,0:T(8,128)(2,1)} %fusion), channel_id=1, source_target_pairs={{0,4},{1,5},{2,6},{3,7},{4,0},{5,1},{6,2},{7,3},{8,12},{9,13},{10,... | collective-permute-start | bytes 5505032 | tf_op jit(solution)/shard_map/ppermute | solution.py:27
  83.0 3.9 %convolution_multiply_fusion.1 = f32[256,3584]{1,0:T(8,128)S(1)} fusion(bf16[256,640]{1,0:T(8,128)(2,1)S(1)} %bitcast.76, bf16[3584,640]{1,0:T(8,128)(2,1)} %param.9), kind=kOutput, calls=%fused_computation.1 | convolution fusion | flops 1175322624 | bytes 8585216 | tf_op jit(solution)/shard_map/dot_general | solution.py:206
  86.9 0.0 copy-start.1
  86.9 0.0 collective-permute-done.13
  87.0 2.7 %fusion.40 = (f16[64,3584]{1,0:T(8,128)(2,1)S(1)}, f16[64,3584]{1,0:T(8,128)(2,1)S(1)}, f16[64,3584]{1,0:T(8,128)(2,1)S(1)}) fusion(f32[4,64,3584]{2,1,0:T(8,128)S(1)} %bitcast.73, s32[]{:T(128)S(6)} %select_n.223, f16[4,64,3584]{2,1,0:T(8,128)(2,1)} %bitcast.21, s32[]{:T(128)S(6)} %select_n.227, s32[]{:T(128)S(6)} %select_n.225), kind=kLoop, calls=%fused_computation.43 | loop fusion | flops 2064384 | bytes 5505036 | tf_op jit(solution)/shard_map/convert_element_type | solution.py:220
  89.6 1.8 %collective-permute-start.14 = (f16[64,3584]{1,0:T(8,128)(2,1)S(1)}, f16[64,3584]{1,0:T(8,128)(2,1)}, u32[]{:S(2)}, u32[]{:S(2)}) collective-permute-start(f16[64,3584]{1,0:T(8,128)(2,1)S(1)} %get-tuple-element.17), channel_id=1, source_target_pairs={{0,8},{1,9},{2,10},{3,11},{4,36},{5,37},{6,38},{7,39},{8,16},{9,17... | collective-permute-start | bytes 1376264 | tf_op jit(solution)/shard_map/ppermute | solution.py:52
  91.4 0.4 collective-permute-start.16
  91.9 2.1 %collective-permute-start.15 = (f16[64,3584]{1,0:T(8,128)(2,1)S(1)}, f16[64,3584]{1,0:T(8,128)(2,1)}, u32[]{:S(2)}, u32[]{:S(2)}) collective-permute-start(f16[64,3584]{1,0:T(8,128)(2,1)S(1)} %get-tuple-element.19), channel_id=1, source_target_pairs={{0,24},{1,25},{2,26},{3,27},{4,100},{5,101},{6,102},{7,103},{8,0},... | collective-permute-start | bytes 1376264 | tf_op jit(solution)/shard_map/ppermute | solution.py:52
  93.9 9.6 %collective-permute-done.14 = f16[64,3584]{1,0:T(8,128)(2,1)} collective-permute-done((f16[64,3584]{1,0:T(8,128)(2,1)S(1)}, f16[64,3584]{1,0:T(8,128)(2,1)}, u32[]{:S(2)}, u32[]{:S(2)}) %collective-permute-start.14) | collective-permute-done | bytes 458784 | tf_op jit(solution)/shard_map/ppermute | solution.py:52
  103.6 0.6 collective-permute-done.15
  104.2 2.0 %fusion.37 = f16[64,3584]{1,0:T(8,128)(2,1)S(1)} fusion(f16[64,3584]{1,0:T(8,128)(2,1)} %collective-permute-done.16, f16[64,3584]{1,0:T(8,128)(2,1)} %collective-permute-done.15, f16[64,3584]{1,0:T(8,128)(2,1)} %collective-permute-done.14, f32[4,64,3584]{2,1,0:T(8,128)} %bitcast.74, s32[]{:T(128)S(6)} %select_n.218, f16[4,64,3584]{2,1,0:T(8,128)(2,1)} %bitcast.21), kind=kLoop, calls=%fused_computation.35 | loop fusion | flops 2064384 | bytes 3211268 | tf_op jit(solution)/shard_map/convert_element_type | solution.py:227
  106.2 0.9 reshape.148
  107.1 4.2 %all-to-all-start.1 = ((f16[16,4,3584]{2,1,0:T(4,128)(2,1)}), f16[16,4,3584]{2,1,0:T(4,128)(2,1)S(1)}, u32[]{:S(2)}, u32[]{:S(2)}) async-start(f16[16,4,3584]{2,1,0:T(4,128)(2,1)} %reshape.148), calls=%async_computation.1 | async-start | bytes 917504 | tf_op jit(solution)/shard_map/all_to_all | solution.py:226
  111.3 6.8 %shard_map.85 = bf16[3584,640]{1,0:T(8,128)(2,1)} custom-call(bf16[512,3584]{1,0:T(8,128)(2,1)} %hidden_ref.1, bf16[512,640]{1,0:T(8,128)(2,1)} %copy-done.2), custom_call_target="tpu_custom_call" | custom-call | tf_op jit(solution)/shard_map/pallas_call | solution.py:101
  118.8 1.8 %all-to-all-done.1 = f16[16,4,3584]{2,1,0:T(4,128)(2,1)S(1)} async-done(((f16[16,4,3584]{2,1,0:T(4,128)(2,1)}), f16[16,4,3584]{2,1,0:T(4,128)(2,1)S(1)}, u32[]{:S(2)}, u32[]{:S(2)}) %all-to-all-start.1) | async-done | bytes 458784 | tf_op jit(solution)/shard_map/all_to_all | solution.py:226
  120.5 0.2 convert_reduce_fusion
  120.7 0.6 broadcast_multiply_fusion
  (31 shorter events, 0.2 us)
Async XLA Ops:
  0.6 5.0 %copy-start = (bf16[512,2048]{1,0:T(8,128)(2,1)S(1)}, bf16[512,2048]{1,0:T(8,128)(2,1)}, u32[]{:S(2)}) copy-start(bf16[512,2048]{1,0:T(8,128)(2,1)} %param.6) | copy-start | bytes 6291460
  0.6 34.5 %all-to-all-start = ((s32[128,4,40]{0,2,1:T(8,128)}), s32[128,4,40]{0,2,1:T(8,128)S(1)}, u32[]{:S(2)}, u32[]{:S(2)}) async-start(s32[128,4,40]{0,2,1:T(8,128)} %bitcast.80), calls=%async_computation | async-start | bytes 163840 | tf_op jit(solution)/shard_map/all_to_all | solution.py:163
  10.0 25.2 %collective-permute-start = (f16[512,640]{1,0:T(8,128)(2,1)}, f16[512,640]{1,0:T(8,128)(2,1)}, u32[]{:S(2)}, u32[]{:S(2)}) collective-permute-start(f16[512,640]{1,0:T(8,128)(2,1)} %fusion.30), channel_id=1, source_target_pairs={{0,2},{1,3},{2,0},{3,1},{4,6},{5,7},{6,4},{7,5},{8,10},{9,11},{10,... | collective-permute-start | bytes 1966088 | tf_op jit(solution)/shard_map/ppermute | solution.py:27
  17.4 24.4 %collective-permute-start.2 = (f16[512,640]{1,0:T(8,128)(2,1)}, f16[512,640]{1,0:T(8,128)(2,1)}, u32[]{:S(2)}, u32[]{:S(2)}) collective-permute-start(f16[512,640]{1,0:T(8,128)(2,1)} %fusion.24), channel_id=1, source_target_pairs={{0,3},{1,0},{2,1},{3,2},{4,7},{5,4},{6,5},{7,6},{8,11},{9,8},{10,9... | collective-permute-start | bytes 1966088 | tf_op jit(solution)/shard_map/ppermute | solution.py:27
  22.6 19.2 %collective-permute-start.1 = (f16[512,640]{1,0:T(8,128)(2,1)}, f16[512,640]{1,0:T(8,128)(2,1)}, u32[]{:S(2)}, u32[]{:S(2)}) collective-permute-start(f16[512,640]{1,0:T(8,128)(2,1)} %fusion.27), channel_id=1, source_target_pairs={{0,1},{1,2},{2,3},{3,0},{4,5},{5,6},{6,7},{7,4},{8,9},{9,10},{10,1... | collective-permute-start | bytes 1966088 | tf_op jit(solution)/shard_map/ppermute | solution.py:27
  23.8 4.7 %copy-start.4 = (bf16[512,3584]{1,0:T(8,128)(2,1)S(1)}, bf16[512,3584]{1,0:T(8,128)(2,1)}, u32[]{:S(2)}) copy-start(bf16[512,3584]{1,0:T(8,128)(2,1)} %hidden_ref.1) | copy-start | bytes 11010052
  28.5 6.0 %copy-start.8 = (pred[640]{0:T(1024)(128)(4,1)S(1)}, pred[640]{0:T(1024)(128)(4,1)}, u32[]{:S(2)}) copy-start(pred[640]{0:T(1024)(128)(4,1)} %get-tuple-element.34) | copy-start | bytes 1924
  28.5 6.0 %copy-start.9 = (pred[640]{0:T(1024)(128)(4,1)S(1)}, pred[640]{0:T(1024)(128)(4,1)}, u32[]{:S(2)}) copy-start(pred[640]{0:T(1024)(128)(4,1)} %get-tuple-element.35) | copy-start | bytes 1924
  28.5 13.2 %copy-start.6 = (s32[512]{0:T(512)S(1)}, s32[512]{0:T(512)}, u32[]{:S(2)}) copy-start(s32[512]{0:T(512)} %param.11) | copy-start | bytes 6148
  41.8 2.9 %copy-start.7 = (f32[512]{0:T(512)S(1)}, f32[512]{0:T(512)}, u32[]{:S(2)}) copy-start(f32[512]{0:T(512)} %get-tuple-element.32) | copy-start | bytes 6148
  44.7 1.2 copy-start.3
  44.7 1.2 copy-start.5
  46.0 2.5 %collective-permute-start.3 = (f32[16,128]{1,0:T(8,128)S(1)}, f32[16,128]{1,0:T(8,128)S(1)}, u32[]{:S(2)}, u32[]{:S(2)}) collective-permute-start(f32[16,128]{1,0:T(8,128)S(1)} %pad_maximum_fusion), channel_id=1, source_target_pairs={{0,4},{1,5},{2,6},{3,7},{4,0},{5,1},{6,2},{7,3},{8,12},{9,13},{10,... | collective-permute-start | bytes 24584 | tf_op jit(solution)/shard_map/ppermute | solution.py:38
  48.5 3.9 %collective-permute-start.6 = (f32[16,128]{1,0:T(8,128)S(1)}, f32[16,128]{1,0:T(8,128)S(1)}, u32[]{:S(2)}, u32[]{:S(2)}) collective-permute-start(f32[16,128]{1,0:T(8,128)S(1)} %pad_maximum_fusion.1), channel_id=1, source_target_pairs={{0,3},{1,2},{2,1},{3,0},{4,7},{5,6},{6,5},{7,4},{8,11},{9,10},{10,... | collective-permute-start | bytes 24584 | tf_op jit(solution)/shard_map/ppermute | solution.py:38
  50.9 2.5 %collective-permute-start.5 = (f32[16,128]{1,0:T(8,128)S(1)}, f32[16,128]{1,0:T(8,128)S(1)}, u32[]{:S(2)}, u32[]{:S(2)}) collective-permute-start(f32[16,128]{1,0:T(8,128)S(1)} %pad_maximum_fusion.1), channel_id=1, source_target_pairs={{0,1},{1,0},{2,3},{3,2},{4,5},{5,4},{6,7},{7,6},{8,9},{9,8},{10,11... | collective-permute-start | bytes 24584 | tf_op jit(solution)/shard_map/ppermute | solution.py:38
  50.9 4.0 %collective-permute-start.4 = (f32[16,128]{1,0:T(8,128)S(1)}, f32[16,128]{1,0:T(8,128)S(1)}, u32[]{:S(2)}, u32[]{:S(2)}) collective-permute-start(f32[16,128]{1,0:T(8,128)S(1)} %pad_maximum_fusion.1), channel_id=1, source_target_pairs={{0,2},{1,3},{2,0},{3,1},{4,6},{5,7},{6,4},{7,5},{8,10},{9,11},{10,... | collective-permute-start | bytes 24584 | tf_op jit(solution)/shard_map/ppermute | solution.py:38
  55.0 4.1 %collective-permute-start.9 = (f32[16,128]{1,0:T(8,128)S(1)}, f32[16,128]{1,0:T(8,128)S(1)}, u32[]{:S(2)}, u32[]{:S(2)}) collective-permute-start(f32[16,128]{1,0:T(8,128)S(1)} %pad_maximum_fusion.2), channel_id=1, source_target_pairs={{0,24},{1,25},{2,26},{3,27},{4,28},{5,29},{6,30},{7,31},{8,16},{9,... | collective-permute-start | bytes 24584 | tf_op jit(solution)/shard_map/ppermute | solution.py:38
  57.8 2.5 %collective-permute-start.8 = (f32[16,128]{1,0:T(8,128)S(1)}, f32[16,128]{1,0:T(8,128)S(1)}, u32[]{:S(2)}, u32[]{:S(2)}) collective-permute-start(f32[16,128]{1,0:T(8,128)S(1)} %pad_maximum_fusion.2), channel_id=1, source_target_pairs={{0,8},{1,9},{2,10},{3,11},{4,12},{5,13},{6,14},{7,15},{8,0},{9,1},... | collective-permute-start | bytes 24584 | tf_op jit(solution)/shard_map/ppermute | solution.py:38
  57.8 4.0 %collective-permute-start.7 = (f32[16,128]{1,0:T(8,128)S(1)}, f32[16,128]{1,0:T(8,128)S(1)}, u32[]{:S(2)}, u32[]{:S(2)}) collective-permute-start(f32[16,128]{1,0:T(8,128)S(1)} %pad_maximum_fusion.2), channel_id=1, source_target_pairs={{0,16},{1,17},{2,18},{3,19},{4,20},{5,21},{6,22},{7,23},{8,24},{9,... | collective-permute-start | bytes 24584 | tf_op jit(solution)/shard_map/ppermute | solution.py:38
  61.9 5.1 %collective-permute-start.12 = (f32[16,128]{1,0:T(8,128)S(1)}, f32[16,128]{1,0:T(8,128)S(1)}, u32[]{:S(2)}, u32[]{:S(2)}) collective-permute-start(f32[16,128]{1,0:T(8,128)S(1)} %pad_maximum_fusion.3), channel_id=1, source_target_pairs={{0,96},{1,97},{2,98},{3,99},{4,100},{5,101},{6,102},{7,103},{8,104... | collective-permute-start | bytes 24584 | tf_op jit(solution)/shard_map/ppermute | solution.py:38
  65.7 2.5 %collective-permute-start.11 = (f32[16,128]{1,0:T(8,128)S(1)}, f32[16,128]{1,0:T(8,128)S(1)}, u32[]{:S(2)}, u32[]{:S(2)}) collective-permute-start(f32[16,128]{1,0:T(8,128)S(1)} %pad_maximum_fusion.3), channel_id=1, source_target_pairs={{0,32},{1,33},{2,34},{3,35},{4,36},{5,37},{6,38},{7,39},{8,40},{9,... | collective-permute-start | bytes 24584 | tf_op jit(solution)/shard_map/ppermute | solution.py:38
  65.7 4.0 %collective-permute-start.10 = (f32[16,128]{1,0:T(8,128)S(1)}, f32[16,128]{1,0:T(8,128)S(1)}, u32[]{:S(2)}, u32[]{:S(2)}) collective-permute-start(f32[16,128]{1,0:T(8,128)S(1)} %pad_maximum_fusion.3), channel_id=1, source_target_pairs={{0,64},{1,65},{2,66},{3,67},{4,68},{5,69},{6,70},{7,71},{8,72},{9,... | collective-permute-start | bytes 24584 | tf_op jit(solution)/shard_map/ppermute | solution.py:38
  72.5 5.4 %copy-start.2 = (bf16[512,640]{1,0:T(8,128)(2,1)}, bf16[512,640]{1,0:T(8,128)(2,1)S(1)}, u32[]{:S(2)}) copy-start(bf16[512,640]{1,0:T(8,128)(2,1)S(1)} %fusion.35.grad_ref) | copy-start | bytes 1966084
  77.9 9.0 %collective-permute-start.13 = (f16[256,3584]{1,0:T(8,128)(2,1)}, f16[256,3584]{1,0:T(8,128)(2,1)}, u32[]{:S(2)}, u32[]{:S(2)}) collective-permute-start(f16[256,3584]{1,0:T(8,128)(2,1)} %fusion), channel_id=1, source_target_pairs={{0,4},{1,5},{2,6},{3,7},{4,0},{5,1},{6,2},{7,3},{8,12},{9,13},{10,... | collective-permute-start | bytes 5505032 | tf_op jit(solution)/shard_map/ppermute | solution.py:27
  86.9 2.7 %copy-start.1 = (f32[256,3584]{1,0:T(8,128)}, f32[256,3584]{1,0:T(8,128)S(1)}, u32[]{:S(2)}) copy-start(f32[256,3584]{1,0:T(8,128)S(1)} %convolution_multiply_fusion.1) | copy-start | bytes 11010052
  89.6 13.9 %collective-permute-start.14 = (f16[64,3584]{1,0:T(8,128)(2,1)S(1)}, f16[64,3584]{1,0:T(8,128)(2,1)}, u32[]{:S(2)}, u32[]{:S(2)}) collective-permute-start(f16[64,3584]{1,0:T(8,128)(2,1)S(1)} %get-tuple-element.17), channel_id=1, source_target_pairs={{0,8},{1,9},{2,10},{3,11},{4,36},{5,37},{6,38},{7,39},{8,16},{9,17... | collective-permute-start | bytes 1376264 | tf_op jit(solution)/shard_map/ppermute | solution.py:52
  91.4 12.1 %collective-permute-start.16 = (f16[64,3584]{1,0:T(8,128)(2,1)S(1)}, f16[64,3584]{1,0:T(8,128)(2,1)}, u32[]{:S(2)}, u32[]{:S(2)}) collective-permute-start(f16[64,3584]{1,0:T(8,128)(2,1)S(1)} %get-tuple-element.18), channel_id=1, source_target_pairs={{0,16},{1,17},{2,18},{3,19},{4,68},{5,69},{6,70},{7,71},{8,24},{9,... | collective-permute-start | bytes 1376264 | tf_op jit(solution)/shard_map/ppermute | solution.py:52
  91.9 12.3 %collective-permute-start.15 = (f16[64,3584]{1,0:T(8,128)(2,1)S(1)}, f16[64,3584]{1,0:T(8,128)(2,1)}, u32[]{:S(2)}, u32[]{:S(2)}) collective-permute-start(f16[64,3584]{1,0:T(8,128)(2,1)S(1)} %get-tuple-element.19), channel_id=1, source_target_pairs={{0,24},{1,25},{2,26},{3,27},{4,100},{5,101},{6,102},{7,103},{8,0},... | collective-permute-start | bytes 1376264 | tf_op jit(solution)/shard_map/ppermute | solution.py:52
  107.1 13.4 %all-to-all-start.1 = ((f16[16,4,3584]{2,1,0:T(4,128)(2,1)}), f16[16,4,3584]{2,1,0:T(4,128)(2,1)S(1)}, u32[]{:S(2)}, u32[]{:S(2)}) async-start(f16[16,4,3584]{2,1,0:T(4,128)(2,1)} %reshape.148), calls=%async_computation.1 | async-start | bytes 917504 | tf_op jit(solution)/shard_map/all_to_all | solution.py:226

commit v2 on v1

--- a/solution.py
+++ b/solution.py
@@ -174,11 +174,19 @@
     picked = jnp.sum(jnp.where(chosen, gap, 0.0), axis=1)
     stats = jnp.concatenate([teacher_lse, student_lse, gap_mean, picked]).reshape(16, 128)
     stats = merged([stats, swap(stats, c=1)])
-    for axis in ("x", "y", "z"):
+    for axis in ("x",):
         far_stats = swap(stats, **{axis: 2})
         near_stats = swap(stats, **{axis: 1})
         next_stats = swap(stats, **{axis: 3})
         stats = merged([stats, far_stats, near_stats, next_stats])
+    every = lax.all_to_all(
+        jnp.broadcast_to(stats[None], (16, 16, 128)), ("z", "y"), 0, 0, tiled=True
+    )
+    top = jnp.max(every[:, :8], axis=0)
+    score = top + jnp.log(jnp.sum(jnp.exp(every[:, :8] - top[None]), axis=0))
+    is_gap = lax.broadcasted_iota(jnp.int32, (8, 128), 0) < 4
+    share = jnp.where(is_gap[None], jnp.exp(every[:, :8] - score[None]), 1.0)
+    stats = jnp.concatenate([score, jnp.sum(share * every[:, 8:], axis=0)])
     lse = stats[:8].reshape(2 * token_total)
     apart = stats[4:8] - stats[:4]
     distill_loss = (
@@ -231,7 +239,7 @@
         axis_index_groups=plane_groups,
         tiled=True,
     )
-    hidden_grad = jnp.sum(wide(last), axis=0) * (1.0 / hidden_scale)
+    hidden_grad = jnp.sum(wide(last) * (1.0 / hidden_scale), axis=0)
     return (distill_loss, head_grad, hidden_grad)
 
 

time: 124 us -> 123 us (level)
  starting transfers between devices: 37.7 us -> 32.7 us
  waiting for transfers between devices: 27.4 us -> 31.7 us
    ppermute x10 -> x4, starting transfers between devices: 14.7 us -> 5.55 us  [swap(): return lax.ppermute(value, every_axis, pairs)]
    all_to_all x0 -> x1, starting transfers between devices: none -> 7.77 us  [per_device(): lax.all_to_all(jnp.broadcast_to(stats[None], (16, 16, 128)), ('z', 'y'),...]
    all_to_all x0 -> x1, waiting for transfers between devices: none -> 6.83 us  [per_device(): lax.all_to_all(jnp.broadcast_to(stats[None], (16, 16, 128)), ('z', 'y'),...]
    ppermute x10 -> x4, waiting for transfers between devices: 8.81 us -> 3.35 us  [swap(): return lax.ppermute(value, every_axis, pairs)]
    ppermute x4, starting transfers between devices: 9.55 us -> 7.99 us  [shift(): return lax.ppermute(value, every_axis, pairs)]
    ppermute x3, waiting for transfers between devices: 10.2 us -> 11.7 us  [core_shift(): return lax.ppermute(value, every_axis, pairs)]
    ppermute x3, starting transfers between devices: 4.3 us -> 2.86 us  [core_shift(): return lax.ppermute(value, every_axis, pairs)]
  transfers between devices with their start and end apart: 19 -> 14, of which waited for: 11 -> 8; matrix products, arithmetic and copies ran while one was open for 24% -> 23% of each run, Pallas kernels for 6% -> 6%
where the time goes in v2:
time: 123 us; the launch traced here: 121 us
  matrix products  35.3 us (29%)
  starting transfers between devices  32.7 us (27%)
  waiting for transfers between devices  31.7 us (26%)
  other arithmetic  10.5 us (9%)
  Pallas kernels  6.84 us (6%)
  between operations  2.62 us (2%)
  local copies, waits for them, and re-layouts  1.68 us (1%)
    dot_general x4, matrix products, teacher_block(): jnp.dot(teacher_hidden, weights, preferred_element_type=jnp.float32)  17.8 us
    ppermute x3, waiting for transfers between devices, core_shift(): return lax.ppermute(value, every_axis, pairs)  11.7 us
    dot_general x2, matrix products, hidden_rows(): lax.dot_general(part, student_head, (((1,), (1,)), ((), ())), preferred_e...  9.2 us
    ppermute x4, starting transfers between devices, shift(): return lax.ppermute(value, every_axis, pairs)  7.99 us
    all_to_all x1, starting transfers between devices, per_device(): lax.all_to_all(jnp.broadcast_to(stats[None], (16, 16, 128)), ('z', 'y'),...  7.77 us
    ppermute x4, waiting for transfers between devices, shift(): return lax.ppermute(value, every_axis, pairs)  7.69 us
    pallas_call x1, Pallas kernels, head_product(): pl.pallas_call(head_kernel, grid=(4,), in_specs=[pl.BlockSpec((tokens, st...  6.84 us
    all_to_all x1, waiting for transfers between devices, per_device(): lax.all_to_all(jnp.broadcast_to(stats[None], (16, 16, 128)), ('z', 'y'),...  6.83 us
  transfers between devices with their start and end apart: 14, of which 8 were waited for; matrix products, arithmetic and copies ran while one was open for 23% of the time, Pallas kernels for 6%

profile of v2, /device:TPU:1, one launch (start us, length us, event | category | flops | bytes accessed | tf_op | source)
XLA Modules:
  0.0 121.3 jit_solution(11892692322147516294)
XLA Ops:
  0.6 0.0 copy-start
  0.6 5.0 %all-to-all-start = ((s32[128,4,40]{0,2,1:T(8,128)}), s32[128,4,40]{0,2,1:T(8,128)S(1)}, u32[]{:S(2)}, u32[]{:S(2)}) async-start(s32[128,4,40]{0,2,1:T(8,128)} %bitcast.80), calls=%async_computation | async-start | bytes 163840 | tf_op jit(solution)/shard_map/all_to_all | solution.py:163
  5.6 0.0 copy-done
  5.6 4.4 %fusion.30 = f16[512,640]{1,0:T(8,128)(2,1)} fusion(bf16[512,2048]{1,0:T(8,128)(2,1)S(1)} %copy-done, bf16[2048,2560]{1,0:T(8,128)(2,1)} %param.7, s32[]{:T(128)S(6)} %select_n.170), kind=kOutput, calls=%fused_computation.24 | convolution fusion | flops 1342504960 | bytes 5373956 | tf_op jit(solution)/shard_map/dot_general | solution.py:147
  10.0 3.0 %collective-permute-start = (f16[512,640]{1,0:T(8,128)(2,1)}, f16[512,640]{1,0:T(8,128)(2,1)}, u32[]{:S(2)}, u32[]{:S(2)}) collective-permute-start(f16[512,640]{1,0:T(8,128)(2,1)} %fusion.30), channel_id=1, source_target_pairs={{0,2},{1,3},{2,0},{3,1},{4,6},{5,7},{6,4},{7,5},{8,10},{9,11},{10,... | collective-permute-start | bytes 1966088 | tf_op jit(solution)/shard_map/ppermute | solution.py:27
  13.0 4.4 %fusion.24 = f16[512,640]{1,0:T(8,128)(2,1)} fusion(bf16[512,2048]{1,0:T(8,128)(2,1)S(1)} %copy-done, bf16[2048,2560]{1,0:T(8,128)(2,1)} %param.7, s32[]{:T(128)S(6)} %select_n.174), kind=kOutput, calls=%fused_computation.22 | convolution fusion | flops 1342504960 | bytes 5373956 | tf_op jit(solution)/shard_map/dot_general | solution.py:147
  17.4 0.8 collective-permute-start.2
  18.2 4.4 %fusion.27 = f16[512,640]{1,0:T(8,128)(2,1)} fusion(bf16[512,2048]{1,0:T(8,128)(2,1)S(1)} %copy-done, bf16[2048,2560]{1,0:T(8,128)(2,1)} %param.7, s32[]{:T(128)S(6)} %select_n.172), kind=kOutput, calls=%fused_computation.23 | convolution fusion | flops 1342504960 | bytes 5373956 | tf_op jit(solution)/shard_map/dot_general | solution.py:147
  22.6 0.6 collective-permute-start.1
  23.2 0.0 copy-start.4
  23.2 4.7 %fusion.12 = f32[512,640]{1,0:T(8,128)} fusion(bf16[512,2048]{1,0:T(8,128)(2,1)S(1)} %copy-done, bf16[2048,2560]{1,0:T(8,128)(2,1)} %param.7, s32[]{:T(128)S(6)} %select_n.168), kind=kOutput, calls=%fused_computation.18 | convolution fusion | flops 1342177280 | bytes 6029316 | tf_op jit(solution)/shard_map/dot_general | solution.py:147
  28.0 0.0 copy-done.4
  28.0 0.0 copy-start.6
  28.0 5.4 %fusion.75 = (f32[512]{0:T(512)S(1)}, f32[512,640]{1,0:T(8,128)S(1)}) fusion(bf16[512,3584]{1,0:T(8,128)(2,1)S(1)} %copy-done.4, bf16[3584,640]{1,0:T(8,128)(2,1)} %param.9), kind=kOutput, calls=%fused_computation.118 | convolution fusion | flops 2349137408 | bytes 9570304 | tf_op jit(solution)/shard_map/dot_general | solution.py:158
  33.4 0.6 fusion.47
  34.0 0.0 all-to-all-done
  34.1 0.0 collective-permute-done
  34.1 7.7 %collective-permute-done.2 = f16[512,640]{1,0:T(8,128)(2,1)} collective-permute-done((f16[512,640]{1,0:T(8,128)(2,1)}, f16[512,640]{1,0:T(8,128)(2,1)}, u32[]{:S(2)}, u32[]{:S(2)}) %collective-permute-start.2) | collective-permute-done | bytes 655392 | tf_op jit(solution)/shard_map/ppermute | solution.py:27
  41.8 0.0 collective-permute-done.1
  41.8 0.0 copy-done.6
  41.8 2.9 %fusion.39 = (f32[512]{0:T(512)S(1)}, f32[512,640]{1,0:T(8,128)S(1)}, pred[512,640]{1,0:T(8,128)(4,1)S(1)}) fusion(f16[512,640]{1,0:T(8,128)(2,1)} %collective-permute-done.2, f16[512,640]{1,0:T(8,128)(2,1)} %collective-permute-done.1, f32[512,640]{1,0:T(8,128)} %fusion.12, f16[512,640]{1,0:T(8,128)(2,1)} %collective-permute-done, s32[512]{0:T(512)S(1)} %copy-done.6, ...), kind=kOutput, calls=%fused_computation.42 | convolution fusion | flops 57230848 | bytes 5057536 | tf_op jit(solution)/shard_map/dot_general | solution.py:123
  44.7 0.0 copy-start.3
  44.7 0.0 copy-start.5
  44.7 1.2 multiply_reduce_fusion
  45.9 0.0 copy-done.3
  45.9 0.0 copy-done.5
  45.9 1.6 %collective-permute-start.3 = (f32[16,128]{1,0:T(8,128)S(1)}, f32[16,128]{1,0:T(8,128)S(1)}, u32[]{:S(2)}, u32[]{:S(2)}) collective-permute-start(f32[16,128]{1,0:T(8,128)S(1)} %pad_maximum_fusion), channel_id=1, source_target_pairs={{0,4},{1,5},{2,6},{3,7},{4,0},{5,1},{6,2},{7,3},{8,12},{9,13},{10,... | collective-permute-start | bytes 24584 | tf_op jit(solution)/shard_map/ppermute | solution.py:38
  47.6 0.8 collective-permute-done.3
  48.4 0.1 fusion.67
  48.5 2.4 %collective-permute-start.6 = (f32[16,128]{1,0:T(8,128)S(1)}, f32[16,128]{1,0:T(8,128)S(1)}, u32[]{:S(2)}, u32[]{:S(2)}) collective-permute-start(f32[16,128]{1,0:T(8,128)S(1)} %pad_maximum_fusion.1), channel_id=1, source_target_pairs={{0,3},{1,2},{2,1},{3,0},{4,7},{5,6},{6,5},{7,4},{8,11},{9,10},{10,... | collective-permute-start | bytes 24584 | tf_op jit(solution)/shard_map/ppermute | solution.py:38
  50.9 0.0 collective-permute-start.5
  50.9 1.5 %collective-permute-start.4 = (f32[16,128]{1,0:T(8,128)S(1)}, f32[16,128]{1,0:T(8,128)S(1)}, u32[]{:S(2)}, u32[]{:S(2)}) collective-permute-start(f32[16,128]{1,0:T(8,128)S(1)} %pad_maximum_fusion.1), channel_id=1, source_target_pairs={{0,2},{1,3},{2,0},{3,1},{4,6},{5,7},{6,4},{7,5},{8,10},{9,11},{10,... | collective-permute-start | bytes 24584 | tf_op jit(solution)/shard_map/ppermute | solution.py:38
  52.4 0.0 collective-permute-done.6
  52.4 1.0 collective-permute-done.5
  53.4 1.5 %collective-permute-done.4 = f32[16,128]{1,0:T(8,128)S(1)} collective-permute-done((f32[16,128]{1,0:T(8,128)S(1)}, f32[16,128]{1,0:T(8,128)S(1)}, u32[]{:S(2)}, u32[]{:S(2)}) %collective-permute-start.4) | collective-permute-done | bytes 8224 | tf_op jit(solution)/shard_map/ppermute | solution.py:38
  54.9 0.1 fusion.65
  55.0 0.7 broadcast_in_dim.54
  55.7 7.8 %all-to-all-start.1 = ((f32[16,16,128]{2,1,0:T(8,128)}), f32[16,16,128]{2,1,0:T(8,128)S(1)}, u32[]{:S(2)}, u32[]{:S(2)}) async-start(f32[16,16,128]{2,1,0:T(8,128)} %broadcast_in_dim.54), calls=%async_computation.1 | async-start | bytes 262144 | tf_op jit(solution)/shard_map/all_to_all | solution.py:182
  63.4 6.8 %all-to-all-done.1 = f32[16,16,128]{2,1,0:T(8,128)S(1)} async-done(((f32[16,16,128]{2,1,0:T(8,128)}), f32[16,16,128]{2,1,0:T(8,128)S(1)}, u32[]{:S(2)}, u32[]{:S(2)}) %all-to-all-start.1) | async-done | bytes 131104 | tf_op jit(solution)/shard_map/all_to_all | solution.py:182
  70.3 0.1 fusion.51
  70.4 0.6 slice_bitcast_fusion.1
  71.0 2.1 %fusion.35.grad_ref = bf16[512,640]{1,0:T(8,128)(2,1)S(1)} fusion(f32[512,640]{1,0:T(8,128)S(1)} %get-tuple-element.29, pred[512,640]{1,0:T(8,128)(4,1)} %copy-done.5, f32[512,640]{1,0:T(8,128)} %copy-done.3, f32[512]{0:T(512)S(1)} %get-tuple-element.21, f32[512]{0:T(512)S(1)} %get-tuple-element.20, s32[640]{0:T(1024)S(1)} %get-tuple-element.35, ...), kind=kLoop, calls=%fused_computation.27 | loop fusion | flops 3604480 | bytes 3613184 | tf_op jit(solution)/shard_map/convert_element_type | solution.py:206
  73.2 0.0 copy-start.2
  73.2 0.1 constant_dynamic-slice_fusion
  73.3 5.3 %fusion = f16[256,3584]{1,0:T(8,128)(2,1)} fusion(bf16[256,640]{1,0:T(8,128)(2,1)S(1)} %bitcast.79, bf16[3584,640]{1,0:T(8,128)(2,1)} %param.9), kind=kOutput, calls=%fused_computation.2 | convolution fusion | flops 1176240128 | bytes 6750208 | tf_op jit(solution)/shard_map/dot_general | solution.py:214
  78.6 0.0 copy-done.2
  78.6 3.5 %collective-permute-start.7 = (f16[256,3584]{1,0:T(8,128)(2,1)}, f16[256,3584]{1,0:T(8,128)(2,1)}, u32[]{:S(2)}, u32[]{:S(2)}) collective-permute-start(f16[256,3584]{1,0:T(8,128)(2,1)} %fusion), channel_id=1, source_target_pairs={{0,4},{1,5},{2,6},{3,7},{4,0},{5,1},{6,2},{7,3},{8,12},{9,13},{10,... | collective-permute-start | bytes 5505032 | tf_op jit(solution)/shard_map/ppermute | solution.py:27
  82.1 3.9 %convolution_multiply_fusion.1 = f32[256,3584]{1,0:T(8,128)S(1)} fusion(bf16[256,640]{1,0:T(8,128)(2,1)S(1)} %bitcast.76, bf16[3584,640]{1,0:T(8,128)(2,1)} %param.9), kind=kOutput, calls=%fused_computation.1 | convolution fusion | flops 1175322624 | bytes 8585216 | tf_op jit(solution)/shard_map/dot_general | solution.py:214
  86.0 0.0 copy-start.1
  86.0 0.0 collective-permute-done.7
  86.0 2.7 %fusion.40 = (f16[64,3584]{1,0:T(8,128)(2,1)S(1)}, f16[64,3584]{1,0:T(8,128)(2,1)S(1)}, f16[64,3584]{1,0:T(8,128)(2,1)S(1)}) fusion(f32[4,64,3584]{2,1,0:T(8,128)S(1)} %bitcast.73, s32[]{:T(128)S(6)} %select_n.196, f16[4,64,3584]{2,1,0:T(8,128)(2,1)} %bitcast.21, s32[]{:T(128)S(6)} %select_n.200, s32[]{:T(128)S(6)} %select_n.198), kind=kLoop, calls=%fused_computation.43 | loop fusion | flops 2064384 | bytes 5505036 | tf_op jit(solution)/shard_map/convert_element_type | solution.py:228
  88.7 0.0 copy-done.1
  88.7 0.1 collective-permute-start.8
  88.8 1.8 %collective-permute-start.10 = (f16[64,3584]{1,0:T(8,128)(2,1)S(1)}, f16[64,3584]{1,0:T(8,128)(2,1)}, u32[]{:S(2)}, u32[]{:S(2)}) collective-permute-start(f16[64,3584]{1,0:T(8,128)(2,1)S(1)} %get-tuple-element.14), channel_id=1, source_target_pairs={{0,16},{1,17},{2,18},{3,19},{4,68},{5,69},{6,70},{7,71},{8,24},{9,... | collective-permute-start | bytes 1376264 | tf_op jit(solution)/shard_map/ppermute | solution.py:52
  90.6 1.0 collective-permute-start.9
  91.6 11.1 %collective-permute-done.8 = f16[64,3584]{1,0:T(8,128)(2,1)} collective-permute-done((f16[64,3584]{1,0:T(8,128)(2,1)S(1)}, f16[64,3584]{1,0:T(8,128)(2,1)}, u32[]{:S(2)}, u32[]{:S(2)}) %collective-permute-start.8) | collective-permute-done | bytes 458784 | tf_op jit(solution)/shard_map/ppermute | solution.py:52
  102.6 0.0 collective-permute-done.10
  102.6 0.6 collective-permute-done.9
  103.3 2.0 %fusion.37 = f16[64,3584]{1,0:T(8,128)(2,1)S(1)} fusion(f16[64,3584]{1,0:T(8,128)(2,1)} %collective-permute-done.10, f16[64,3584]{1,0:T(8,128)(2,1)} %collective-permute-done.9, f16[64,3584]{1,0:T(8,128)(2,1)} %collective-permute-done.8, f32[4,64,3584]{2,1,0:T(8,128)} %bitcast.74, s32[]{:T(128)S(6)} %select_n.191, f16[4,64,3584]{2,1,0:T(8,128)(2,1)} %bitcast.21), kind=kLoop, calls=%fused_computation.35 | loop fusion | flops 2064384 | bytes 3211268 | tf_op jit(solution)/shard_map/convert_element_type | solution.py:235
  105.3 0.9 reshape.156
  106.2 3.6 %all-to-all-start.2 = ((f16[16,4,3584]{2,1,0:T(4,128)(2,1)}), f16[16,4,3584]{2,1,0:T(4,128)(2,1)S(1)}, u32[]{:S(2)}, u32[]{:S(2)}) async-start(f16[16,4,3584]{2,1,0:T(4,128)(2,1)} %reshape.156), calls=%async_computation.2 | async-start | bytes 917504 | tf_op jit(solution)/shard_map/all_to_all | solution.py:234
  109.7 6.8 %shard_map.85 = bf16[3584,640]{1,0:T(8,128)(2,1)} custom-call(bf16[512,3584]{1,0:T(8,128)(2,1)} %hidden_ref.1, bf16[512,640]{1,0:T(8,128)(2,1)} %copy-done.2), custom_call_target="tpu_custom_call" | custom-call | tf_op jit(solution)/shard_map/pallas_call | solution.py:101
  117.2 2.1 %all-to-all-done.2 = f16[16,4,3584]{2,1,0:T(4,128)(2,1)S(1)} async-done(((f16[16,4,3584]{2,1,0:T(4,128)(2,1)}), f16[16,4,3584]{2,1,0:T(4,128)(2,1)S(1)}, u32[]{:S(2)}, u32[]{:S(2)}) %all-to-all-start.2) | async-done | bytes 458784 | tf_op jit(solution)/shard_map/all_to_all | solution.py:234
  119.3 0.9 multiply_reduce_fusion.1
  (16 shorter events, 0.2 us)
Async XLA Ops:
  0.6 5.0 %copy-start = (bf16[512,2048]{1,0:T(8,128)(2,1)S(1)}, bf16[512,2048]{1,0:T(8,128)(2,1)}, u32[]{:S(2)}) copy-start(bf16[512,2048]{1,0:T(8,128)(2,1)} %param.6) | copy-start | bytes 6291460
  0.6 33.4 %all-to-all-start = ((s32[128,4,40]{0,2,1:T(8,128)}), s32[128,4,40]{0,2,1:T(8,128)S(1)}, u32[]{:S(2)}, u32[]{:S(2)}) async-start(s32[128,4,40]{0,2,1:T(8,128)} %bitcast.80), calls=%async_computation | async-start | bytes 163840 | tf_op jit(solution)/shard_map/all_to_all | solution.py:163
  10.0 24.1 %collective-permute-start = (f16[512,640]{1,0:T(8,128)(2,1)}, f16[512,640]{1,0:T(8,128)(2,1)}, u32[]{:S(2)}, u32[]{:S(2)}) collective-permute-start(f16[512,640]{1,0:T(8,128)(2,1)} %fusion.30), channel_id=1, source_target_pairs={{0,2},{1,3},{2,0},{3,1},{4,6},{5,7},{6,4},{7,5},{8,10},{9,11},{10,... | collective-permute-start | bytes 1966088 | tf_op jit(solution)/shard_map/ppermute | solution.py:27
  17.4 24.4 %collective-permute-start.2 = (f16[512,640]{1,0:T(8,128)(2,1)}, f16[512,640]{1,0:T(8,128)(2,1)}, u32[]{:S(2)}, u32[]{:S(2)}) collective-permute-start(f16[512,640]{1,0:T(8,128)(2,1)} %fusion.24), channel_id=1, source_target_pairs={{0,3},{1,0},{2,1},{3,2},{4,7},{5,4},{6,5},{7,6},{8,11},{9,8},{10,9... | collective-permute-start | bytes 1966088 | tf_op jit(solution)/shard_map/ppermute | solution.py:27
  22.6 19.2 %collective-permute-start.1 = (f16[512,640]{1,0:T(8,128)(2,1)}, f16[512,640]{1,0:T(8,128)(2,1)}, u32[]{:S(2)}, u32[]{:S(2)}) collective-permute-start(f16[512,640]{1,0:T(8,128)(2,1)} %fusion.27), channel_id=1, source_target_pairs={{0,1},{1,2},{2,3},{3,0},{4,5},{5,6},{6,7},{7,4},{8,9},{9,10},{10,1... | collective-permute-start | bytes 1966088 | tf_op jit(solution)/shard_map/ppermute | solution.py:27
  23.2 4.7 %copy-start.4 = (bf16[512,3584]{1,0:T(8,128)(2,1)S(1)}, bf16[512,3584]{1,0:T(8,128)(2,1)}, u32[]{:S(2)}) copy-start(bf16[512,3584]{1,0:T(8,128)(2,1)} %hidden_ref.1) | copy-start | bytes 11010052
  28.0 13.8 %copy-start.6 = (s32[512]{0:T(512)S(1)}, s32[512]{0:T(512)}, u32[]{:S(2)}) copy-start(s32[512]{0:T(512)} %param.11) | copy-start | bytes 6148
  44.7 1.2 %copy-start.3 = (f32[512,640]{1,0:T(8,128)}, f32[512,640]{1,0:T(8,128)S(1)}, u32[]{:S(2)}) copy-start(f32[512,640]{1,0:T(8,128)S(1)} %get-tuple-element.12) | copy-start | bytes 3932164
  44.7 1.2 copy-start.5
  45.9 2.5 %collective-permute-start.3 = (f32[16,128]{1,0:T(8,128)S(1)}, f32[16,128]{1,0:T(8,128)S(1)}, u32[]{:S(2)}, u32[]{:S(2)}) collective-permute-start(f32[16,128]{1,0:T(8,128)S(1)} %pad_maximum_fusion), channel_id=1, source_target_pairs={{0,4},{1,5},{2,6},{3,7},{4,0},{5,1},{6,2},{7,3},{8,12},{9,13},{10,... | collective-permute-start | bytes 24584 | tf_op jit(solution)/shard_map/ppermute | solution.py:38
  48.5 3.9 %collective-permute-start.6 = (f32[16,128]{1,0:T(8,128)S(1)}, f32[16,128]{1,0:T(8,128)S(1)}, u32[]{:S(2)}, u32[]{:S(2)}) collective-permute-start(f32[16,128]{1,0:T(8,128)S(1)} %pad_maximum_fusion.1), channel_id=1, source_target_pairs={{0,3},{1,2},{2,1},{3,0},{4,7},{5,6},{6,5},{7,4},{8,11},{9,10},{10,... | collective-permute-start | bytes 24584 | tf_op jit(solution)/shard_map/ppermute | solution.py:38
  50.9 2.5 %collective-permute-start.5 = (f32[16,128]{1,0:T(8,128)S(1)}, f32[16,128]{1,0:T(8,128)S(1)}, u32[]{:S(2)}, u32[]{:S(2)}) collective-permute-start(f32[16,128]{1,0:T(8,128)S(1)} %pad_maximum_fusion.1), channel_id=1, source_target_pairs={{0,1},{1,0},{2,3},{3,2},{4,5},{5,4},{6,7},{7,6},{8,9},{9,8},{10,11... | collective-permute-start | bytes 24584 | tf_op jit(solution)/shard_map/ppermute | solution.py:38
  50.9 4.0 %collective-permute-start.4 = (f32[16,128]{1,0:T(8,128)S(1)}, f32[16,128]{1,0:T(8,128)S(1)}, u32[]{:S(2)}, u32[]{:S(2)}) collective-permute-start(f32[16,128]{1,0:T(8,128)S(1)} %pad_maximum_fusion.1), channel_id=1, source_target_pairs={{0,2},{1,3},{2,0},{3,1},{4,6},{5,7},{6,4},{7,5},{8,10},{9,11},{10,... | collective-permute-start | bytes 24584 | tf_op jit(solution)/shard_map/ppermute | solution.py:38
  55.7 14.6 %all-to-all-start.1 = ((f32[16,16,128]{2,1,0:T(8,128)}), f32[16,16,128]{2,1,0:T(8,128)S(1)}, u32[]{:S(2)}, u32[]{:S(2)}) async-start(f32[16,16,128]{2,1,0:T(8,128)} %broadcast_in_dim.54), calls=%async_computation.1 | async-start | bytes 262144 | tf_op jit(solution)/shard_map/all_to_all | solution.py:182
  73.2 5.4 %copy-start.2 = (bf16[512,640]{1,0:T(8,128)(2,1)}, bf16[512,640]{1,0:T(8,128)(2,1)S(1)}, u32[]{:S(2)}) copy-start(bf16[512,640]{1,0:T(8,128)(2,1)S(1)} %fusion.35.grad_ref) | copy-start | bytes 1966084
  78.6 7.5 %collective-permute-start.7 = (f16[256,3584]{1,0:T(8,128)(2,1)}, f16[256,3584]{1,0:T(8,128)(2,1)}, u32[]{:S(2)}, u32[]{:S(2)}) collective-permute-start(f16[256,3584]{1,0:T(8,128)(2,1)} %fusion), channel_id=1, source_target_pairs={{0,4},{1,5},{2,6},{3,7},{4,0},{5,1},{6,2},{7,3},{8,12},{9,13},{10,... | collective-permute-start | bytes 5505032 | tf_op jit(solution)/shard_map/ppermute | solution.py:27
  86.0 2.7 %copy-start.1 = (f32[256,3584]{1,0:T(8,128)}, f32[256,3584]{1,0:T(8,128)S(1)}, u32[]{:S(2)}) copy-start(f32[256,3584]{1,0:T(8,128)S(1)} %convolution_multiply_fusion.1) | copy-start | bytes 11010052
  88.7 13.9 %collective-permute-start.8 = (f16[64,3584]{1,0:T(8,128)(2,1)S(1)}, f16[64,3584]{1,0:T(8,128)(2,1)}, u32[]{:S(2)}, u32[]{:S(2)}) collective-permute-start(f16[64,3584]{1,0:T(8,128)(2,1)S(1)} %get-tuple-element.13), channel_id=1, source_target_pairs={{0,8},{1,9},{2,10},{3,11},{4,36},{5,37},{6,38},{7,39},{8,16},{9,17... | collective-permute-start | bytes 1376264 | tf_op jit(solution)/shard_map/ppermute | solution.py:52
  88.8 13.8 %collective-permute-start.10 = (f16[64,3584]{1,0:T(8,128)(2,1)S(1)}, f16[64,3584]{1,0:T(8,128)(2,1)}, u32[]{:S(2)}, u32[]{:S(2)}) collective-permute-start(f16[64,3584]{1,0:T(8,128)(2,1)S(1)} %get-tuple-element.14), channel_id=1, source_target_pairs={{0,16},{1,17},{2,18},{3,19},{4,68},{5,69},{6,70},{7,71},{8,24},{9,... | collective-permute-start | bytes 1376264 | tf_op jit(solution)/shard_map/ppermute | solution.py:52
  90.6 12.7 %collective-permute-start.9 = (f16[64,3584]{1,0:T(8,128)(2,1)S(1)}, f16[64,3584]{1,0:T(8,128)(2,1)}, u32[]{:S(2)}, u32[]{:S(2)}) collective-permute-start(f16[64,3584]{1,0:T(8,128)(2,1)S(1)} %get-tuple-element.15), channel_id=1, source_target_pairs={{0,24},{1,25},{2,26},{3,27},{4,100},{5,101},{6,102},{7,103},{8,0},... | collective-permute-start | bytes 1376264 | tf_op jit(solution)/shard_map/ppermute | solution.py:52
  106.2 13.2 %all-to-all-start.2 = ((f16[16,4,3584]{2,1,0:T(4,128)(2,1)}), f16[16,4,3584]{2,1,0:T(4,128)(2,1)S(1)}, u32[]{:S(2)}, u32[]{:S(2)}) async-start(f16[16,4,3584]{2,1,0:T(4,128)(2,1)} %reshape.156), calls=%async_computation.2 | async-start | bytes 917504 | tf_op jit(solution)/shard_map/all_to_all | solution.py:234
